TPU v7x, 512 devices: a whole 4x8x8 slice. The times are simulated.
512 devices in a mesh: rows: 64 (over y, z), grp: 8 (over x, core).
Axes of the slice: x: 4, y: 8, z: 8, core: 2. Of those that a mesh axis runs over, the one named last changes fastest.
Arguments:
- basis: float32 [64, 2097152], P(None, ('rows', 'grp'))
- values: float32 [64], replicated, may hold values from 0.5 to 20
- archive: bfloat16 [64, 2097152], P('grp', 'rows')
- window_ids: int32 [32], replicated, may hold values from 0 to 63, as said below
Outputs:
- filtered: float32 [96, 2097152], P(None, ('rows', 'grp'))
- projector: float32 [96, 96], replicated
- novelty: float32 [32], replicated
Inputs may be any that keep to these rules, and one draw needn't show every extreme that they name: `window_ids`: distinct; 0 and 63 are always among them.
All inputs are finite; a program needn't handle non-finite values.
Results may differ from a plain program's by a relative error of at most 0.0003.
Values may be sent and summed in bfloat16 or wider, within the bound.
No kernel may reach another device: no remote copies, remote signals or barrier semaphores. Data moves between devices by JAX's collectives and lax.ppermute only.
A program may use at most 64 MiB of HBM per device.

v0:
```python
import math

import jax
import jax.numpy as jnp
from jax import lax
from jax.sharding import PartitionSpec as P

NEWTON = 10


HIGH = lax.Precision.HIGHEST


def spectral(core):
    width = core.shape[0]
    identity = jnp.eye(width, dtype=jnp.float32)
    square = jnp.dot(core, core.T, precision=HIGH)
    total = jnp.trace(square)
    shifted = (square - total / width * identity) / total
    for iteration in range(NEWTON):
        cubed = jnp.dot(jnp.dot(shifted, shifted, precision=HIGH), shifted, precision=HIGH)
        shifted = 1.5 * shifted - 0.5 * cubed
    return 0.5 * (identity + shifted)


def inverse_lower(gram):
    factor = jnp.linalg.cholesky(gram)
    identity = jnp.eye(gram.shape[0], dtype=jnp.float32)
    return (factor, jax.scipy.linalg.solve_triangular(factor, identity, lower=True))


def per_device(basis, values, archive, window_ids):
    mode_count = basis.shape[0]
    window_count = window_ids.shape[0]
    local_rows = basis.shape[1]
    total_rows = local_rows * lax.axis_size("rows") * lax.axis_size("grp")
    everything = lax.all_to_all(archive, "grp", split_axis=1, concat_axis=0, tiled=True)
    picker = (
        window_ids[:, None] == jnp.arange(everything.shape[0], dtype=jnp.int32)[None, :]
    ).astype(jnp.bfloat16)
    gathered = jnp.dot(picker, everything, preferred_element_type=jnp.float32)
    columns = gathered * (1.0 / math.sqrt(total_rows))
    proj_part = jnp.einsum("kr,pr->kp", basis, columns, precision=HIGH)
    energy_part = jnp.sum(columns * columns, axis=1)
    projection, energy = lax.psum((proj_part, energy_part), ("rows", "grp"))
    resid = columns - jnp.einsum("kp,kr->pr", projection, basis, precision=HIGH)
    gram_one = lax.psum(jnp.einsum("pr,qr->pq", resid, resid, precision=HIGH), ("rows", "grp"))
    factor_one, inverse_one = inverse_lower(gram_one)
    first = jnp.dot(inverse_one, resid, precision=HIGH)
    gram_two = lax.psum(jnp.einsum("pr,qr->pq", first, first, precision=HIGH), ("rows", "grp"))
    factor_two, inverse_two = inverse_lower(gram_two)
    ortho = jnp.dot(inverse_two, first, precision=HIGH)
    upper = jnp.dot(factor_two.T, factor_one.T, precision=HIGH)
    top_rows = jnp.concatenate([jnp.diag(values), projection], axis=1)
    low_rows = jnp.concatenate([jnp.zeros((window_count, mode_count), jnp.float32), upper], axis=1)
    core = jnp.concatenate([top_rows, low_rows], axis=0)
    projector = spectral(core)
    weights = jnp.dot(core.T, projector, precision=HIGH)
    stacked = jnp.concatenate([basis, ortho], axis=0)
    filtered = jnp.dot(weights, stacked, precision=HIGH) * math.sqrt(total_rows)
    novelty = jnp.diagonal(gram_one) / energy
    return (filtered, projector, novelty)


def solution(mesh):
    placed = (P(None, ("rows", "grp")), P(), P("grp", "rows"), P())
    return jax.shard_map(
        per_device,
        mesh=mesh,
        in_specs=placed,
        out_specs=(P(None, ("rows", "grp")), P(), P()),
        check_vma=False,
    )
```

profile of v0, /device:TPU:1, one launch (start us, length us, event | category | flops | bytes accessed | tf_op | source)
XLA Modules:
  0.0 339.9 jit_solution(17657873917726056590)
XLA Ops:
  0.6 10.4 %all-to-all-start = ((bf16[8,8,4096]{2,0,1:T(8,128)(2,1)}), bf16[8,8,4096]{2,0,1:T(8,128)(2,1)S(1)}, u32[]{:S(2)}, u32[]{:S(2)}) async-start(bf16[8,8,4096]{2,0,1:T(8,128)(2,1)} %bitcast.81), calls=%async_computation | async-start | bytes 1048576 | tf_op jit(solution)/shard_map/all_to_all | solution.py:37
  11.0 0.7 fusion.16
  11.8 8.6 %all-to-all-done = bf16[8,8,4096]{2,0,1:T(8,128)(2,1)S(1)} async-done(((bf16[8,8,4096]{2,0,1:T(8,128)(2,1)}), bf16[8,8,4096]{2,0,1:T(8,128)(2,1)S(1)}, u32[]{:S(2)}, u32[]{:S(2)}) %all-to-all-start) | async-done | bytes 524320 | tf_op jit(solution)/shard_map/all_to_all | solution.py:37
  20.4 1.0 multiply_reduce_fusion
  21.4 1.0 convolution_bitcast_fusion
  22.4 99.3 %psum.28 = f32[64,32]{0,1:T(8,128)S(1)} all-reduce(f32[64,32]{0,1:T(8,128)S(1)} %convolution_bitcast_fusion), channel_id=1, replica_groups=mesh['rows'=64,'grp'=8] {'rows','grp'}, use_global_device_ids=true, to_apply=%region_0.0 | all-reduce | flops 2048 | bytes 16384 | tf_op jit(solution)/shard_map/psum | solution.py:45
  121.7 0.6 convolution_subtract_fusion
  122.4 0.6 fusion.51
  123.0 94.3 %psum.29 = f32[32,32]{0,1:T(8,128)S(1)} all-reduce(f32[32,32]{0,1:T(8,128)S(1)} %fusion.51), channel_id=1, replica_groups=mesh['rows'=64,'grp'=8] {'rows','grp'}, use_global_device_ids=true, to_apply=%region_1.0 | all-reduce | flops 1024 | bytes 8192 | tf_op jit(solution)/shard_map/psum | solution.py:47
  217.3 2.9 cholesky.44
  220.3 0.6 compare_reduce_fusion.1
  220.9 0.7 fusion.29
  221.6 2.4 custom-call.8
  224.0 0.2 fusion.19
  224.3 0.6 fusion.52
  224.8 0.6 fusion.53
  225.4 94.5 %all-reduce.1 = (f32[32,32]{0,1:T(8,128)S(1)}, f32[32]{0:T(128)S(1)}) all-reduce(f32[32,32]{0,1:T(8,128)S(1)} %fusion.53, f32[32]{0:T(128)S(1)} %get-tuple-element.7), channel_id=1, replica_groups=mesh['rows'=64,'grp'=8] {'rows','grp'}, use_global_device_ids=true, to_apply=%region_4.0 | all-reduce | flops 1056 | bytes 8448 | tf_op jit(solution)/shard_map/psum | solution.py:50
  320.0 2.9 cholesky.55
  323.0 0.6 compare_reduce_fusion
  323.6 1.5 fusion.30
  325.1 0.7 select_bitcast_fusion
  325.8 0.7 gather_fusion
  326.5 2.4 custom-call.9
  328.9 0.2 fusion.17
  329.2 0.6 fusion.63
  329.8 0.9 select_reduce_fusion
  331.3 0.8 fusion.34
  332.2 0.8 fusion.14
  333.0 0.2 fusion.54
  333.2 0.2 fusion.13
  333.4 0.2 fusion.55
  333.6 0.2 fusion.12
  333.8 0.2 fusion.56
  333.9 0.2 fusion.11
  334.1 0.2 fusion.57
  334.3 0.2 fusion.10
  334.5 0.2 fusion.58
  334.7 0.2 fusion.9
  334.9 0.2 fusion.59
  335.1 0.2 fusion.8
  335.5 0.2 fusion.7
  335.6 0.2 fusion.61
  335.8 0.2 fusion.6
  336.0 0.2 fusion.62
  336.2 0.2 fusion.5
  336.4 0.3 fusion.32
  336.7 0.5 div.21
  337.3 2.6 convolution_multiply_fusion
  (13 shorter events, 0.5 us)
Async XLA Ops:
  0.6 20.8 %copy-start = (f32[64,4096]{1,0:T(8,128)S(1)}, f32[64,4096]{1,0:T(8,128)}, u32[]{:S(2)}) copy-start(f32[64,4096]{1,0:T(8,128)} %param.7) | copy-start | bytes 3145732
  0.6 19.8 %all-to-all-start = ((bf16[8,8,4096]{2,0,1:T(8,128)(2,1)}), bf16[8,8,4096]{2,0,1:T(8,128)(2,1)S(1)}, u32[]{:S(2)}, u32[]{:S(2)}) async-start(bf16[8,8,4096]{2,0,1:T(8,128)(2,1)} %bitcast.81), calls=%async_computation | async-start | bytes 1048576 | tf_op jit(solution)/shard_map/all_to_all | solution.py:37
  336.4 3.5 %copy-start.1 = (f32[96,96]{1,0:T(8,128)}, f32[96,96]{1,0:T(8,128)S(1)}, u32[]{:S(2)}) copy-start(f32[96,96]{1,0:T(8,128)S(1)} %fusion.5) | copy-start | bytes 110596
where the time goes:
time: 341 us; the launch traced here: 340 us
  blocking collectives  288 us (84%)
  matrix products  15.7 us (5%)
  other arithmetic  14.7 us (4%)
  starting transfers between devices  10.4 us (3%)
  waiting for transfers between devices  8.64 us (3%)
    psum x1, blocking collectives, per_device(): projection, energy = lax.psum((proj_part, energy_part), ('rows', 'grp'))  99.3 us
    psum x1, blocking collectives, per_device(): lax.psum(jnp.einsum('pr,qr->pq', first, first, precision=HIGH), ('rows',...  94.5 us
    psum x1, blocking collectives, per_device(): lax.psum(jnp.einsum('pr,qr->pq', resid, resid, precision=HIGH), ('rows',...  94.3 us
    all_to_all x1, starting transfers between devices, per_device(): lax.all_to_all(archive, 'grp', split_axis=1, concat_axis=0, tiled=True)  10.4 us
    all_to_all x1, waiting for transfers between devices, per_device(): lax.all_to_all(archive, 'grp', split_axis=1, concat_axis=0, tiled=True)  8.64 us
    another operation x6, other arithmetic, inverse_lower(): factor = jnp.linalg.cholesky(gram)  7.19 us
  transfers between devices with their start and end apart: 1, of which 1 were waited for; matrix products, arithmetic and copies ran while one was open for 0% of the time, Pallas kernels for 0%

commit v1 on v0

--- a/solution.py
+++ b/solution.py
@@ -3,12 +3,11 @@
 import jax
 import jax.numpy as jnp
 from jax import lax
-from jax.sharding import PartitionSpec as P
+from jax.sharding import Mesh, PartitionSpec as P
 
 NEWTON = 10
-
-
 HIGH = lax.Precision.HIGHEST
+ALL = ("y", "z", "x", "c")
 
 
 def spectral(core):
@@ -29,12 +28,26 @@
     return (factor, jax.scipy.linalg.solve_triangular(factor, identity, lower=True))
 
 
+def sum_over(block, axes):
+    count = 1
+    for name in axes:
+        count *= lax.axis_size(name)
+    copies = jnp.broadcast_to(block[None], (count,) + block.shape)
+    return jnp.sum(lax.all_to_all(copies, axes, 0, 0, tiled=True), axis=0)
+
+
+def total_sum(block):
+    return sum_over(sum_over(block, ("y", "x")), ("z", "c"))
+
+
 def per_device(basis, values, archive, window_ids):
     mode_count = basis.shape[0]
     window_count = window_ids.shape[0]
     local_rows = basis.shape[1]
-    total_rows = local_rows * lax.axis_size("rows") * lax.axis_size("grp")
-    everything = lax.all_to_all(archive, "grp", split_axis=1, concat_axis=0, tiled=True)
+    total_rows = local_rows
+    for name in ALL:
+        total_rows *= lax.axis_size(name)
+    everything = lax.all_to_all(archive, ("x", "c"), split_axis=1, concat_axis=0, tiled=True)
     picker = (
         window_ids[:, None] == jnp.arange(everything.shape[0], dtype=jnp.int32)[None, :]
     ).astype(jnp.bfloat16)
@@ -42,12 +55,17 @@
     columns = gathered * (1.0 / math.sqrt(total_rows))
     proj_part = jnp.einsum("kr,pr->kp", basis, columns, precision=HIGH)
     energy_part = jnp.sum(columns * columns, axis=1)
-    projection, energy = lax.psum((proj_part, energy_part), ("rows", "grp"))
+    packed = jnp.concatenate([proj_part, energy_part[None, :], jnp.zeros((7, window_count), jnp.float32)], axis=0)
+    packed = total_sum(packed.reshape(-1, 128)).reshape(packed.shape)
+    projection = packed[:mode_count]
+    energy = packed[mode_count]
     resid = columns - jnp.einsum("kp,kr->pr", projection, basis, precision=HIGH)
-    gram_one = lax.psum(jnp.einsum("pr,qr->pq", resid, resid, precision=HIGH), ("rows", "grp"))
+    gram_one = jnp.einsum("pr,qr->pq", resid, resid, precision=HIGH)
+    gram_one = total_sum(gram_one.reshape(-1, 128)).reshape(gram_one.shape)
     factor_one, inverse_one = inverse_lower(gram_one)
     first = jnp.dot(inverse_one, resid, precision=HIGH)
-    gram_two = lax.psum(jnp.einsum("pr,qr->pq", first, first, precision=HIGH), ("rows", "grp"))
+    gram_two = jnp.einsum("pr,qr->pq", first, first, precision=HIGH)
+    gram_two = total_sum(gram_two.reshape(-1, 128)).reshape(gram_two.shape)
     factor_two, inverse_two = inverse_lower(gram_two)
     ortho = jnp.dot(inverse_two, first, precision=HIGH)
     upper = jnp.dot(factor_two.T, factor_one.T, precision=HIGH)
@@ -63,11 +81,12 @@
 
 
 def solution(mesh):
-    placed = (P(None, ("rows", "grp")), P(), P("grp", "rows"), P())
+    fine = Mesh(mesh.devices.reshape(8, 8, 4, 2), ALL)
+    placed = (P(None, ALL), P(), P(("x", "c"), ("y", "z")), P())
     return jax.shard_map(
         per_device,
-        mesh=mesh,
+        mesh=fine,
         in_specs=placed,
-        out_specs=(P(None, ("rows", "grp")), P(), P()),
+        out_specs=(P(None, ALL), P(), P()),
         check_vma=False,
     )

time: 341 us -> 145 us (0.43)
  blocking collectives: 288 us -> 65.2 us
  waiting for transfers between devices: 8.64 us -> 25.6 us
  starting transfers between devices: 10.4 us -> 19.1 us
    psum x3 -> x0, blocking collectives: 288 us -> none  [the longest x1 99.3 us: per_device(): projection, energy = lax.psum((proj_part, energy_part), ('rows', 'grp'))]
    all_to_all x0 -> x4, blocking collectives: none -> 65.2 us  [sum_over(): return jnp.sum(lax.all_to_all(copies, axes, 0, 0, tiled=True), axis=0)]
    all_to_all x1 -> x3, waiting for transfers between devices: 8.64 us -> 25.6 us  [the longest x2 16.3 us: sum_over(): return jnp.sum(lax.all_to_all(copies, axes, 0, 0, tiled=True), axis=0)]
    all_to_all x1 -> x3, starting transfers between devices: 10.4 us -> 19.1 us  [the longest x1 10.4 us: per_device(): lax.all_to_all(archive, ('x', 'c'), split_axis=1, concat_axis=0, tiled=True)]
  transfers between devices with their start and end apart: 1 -> 3, of which waited for: 1 -> 3; matrix products, arithmetic and copies ran while one was open for 0% -> 1% of each run, Pallas kernels for 0% -> 0%
where the time goes in v1:
time: 145 us; the launch traced here: 144 us
  blocking collectives  65.2 us (45%)
  waiting for transfers between devices  25.6 us (18%)
  starting transfers between devices  19.1 us (13%)
  matrix products  15.7 us (11%)
  other arithmetic  14.3 us (10%)
  local copies, waits for them, and re-layouts  3.03 us (2%)
  between operations  1.55 us (1%)
    all_to_all x4, blocking collectives, sum_over(): return jnp.sum(lax.all_to_all(copies, axes, 0, 0, tiled=True), axis=0)  65.2 us
    all_to_all x2, waiting for transfers between devices, sum_over(): return jnp.sum(lax.all_to_all(copies, axes, 0, 0, tiled=True), axis=0)  16.3 us
    all_to_all x1, starting transfers between devices, per_device(): lax.all_to_all(archive, ('x', 'c'), split_axis=1, concat_axis=0, tiled=True)  10.4 us
    all_to_all x1, waiting for transfers between devices, per_device(): lax.all_to_all(archive, ('x', 'c'), split_axis=1, concat_axis=0, tiled=True)  9.3 us
    all_to_all x2, starting transfers between devices, sum_over(): return jnp.sum(lax.all_to_all(copies, axes, 0, 0, tiled=True), axis=0)  8.75 us
    another operation x6, other arithmetic, inverse_lower(): factor = jnp.linalg.cholesky(gram)  7.19 us
    another operation x4, other arithmetic, inverse_lower(): jax.scipy.linalg.solve_triangular(factor, identity, lower=True)  6.19 us
  transfers between devices with their start and end apart: 3, of which 3 were waited for; matrix products, arithmetic and copies ran while one was open for 1% of the time, Pallas kernels for 0%

profile of v1, /device:TPU:1, one launch (start us, length us, event | category | flops | bytes accessed | tf_op | source)
XLA Modules:
  0.0 144.5 jit_solution(14259944264442497772)
XLA Ops:
  0.6 10.4 %all-to-all-start = ((bf16[8,8,4096]{2,0,1:T(8,128)(2,1)}), bf16[8,8,4096]{2,0,1:T(8,128)(2,1)S(1)}, u32[]{:S(2)}, u32[]{:S(2)}) async-start(bf16[8,8,4096]{2,0,1:T(8,128)(2,1)} %bitcast.86), calls=%async_computation | async-start | bytes 1048576 | tf_op jit(solution)/shard_map/all_to_all | solution.py:50
  11.1 9.3 %all-to-all-done = bf16[8,8,4096]{2,0,1:T(8,128)(2,1)S(1)} async-done(((bf16[8,8,4096]{2,0,1:T(8,128)(2,1)}), bf16[8,8,4096]{2,0,1:T(8,128)(2,1)S(1)}, u32[]{:S(2)}, u32[]{:S(2)}) %all-to-all-start) | async-done | bytes 524320 | tf_op jit(solution)/shard_map/all_to_all | solution.py:50
  20.4 1.0 multiply_reduce_fusion
  21.5 1.0 convolution_bitcast_fusion
  22.8 16.9 %all_to_all.49 = f32[32,18,128]{2,1,0:T(8,128)S(1)} all-to-all(f32[32,18,128]{2,1,0:T(8,128)S(1)} %broadcast_in_dim.80), channel_id=1, replica_groups=mesh['y'=8,'z'=8,'x'=4,'c'=2] {'y','x'}, dimensions={0} | all-to-all | bytes 589824 | tf_op jit(solution)/shard_map/all_to_all | solution.py:36
  39.7 22.9 %all_to_all.50 = f32[16,18,128]{2,1,0:T(8,128)S(1)} all-to-all(f32[16,18,128]{2,1,0:T(8,128)S(1)} %broadcast_in_dim.81), channel_id=1, replica_groups=mesh['y'=8,'z'=8,'x'=4,'c'=2] {'z','c'}, dimensions={0} | all-to-all | bytes 294912 | tf_op jit(solution)/shard_map/all_to_all | solution.py:36
  62.8 0.7 convolution_subtract_fusion
  63.4 0.6 fusion.52
  64.1 13.6 %all_to_all.51 = f32[32,8,128]{2,1,0:T(8,128)S(1)} all-to-all(f32[32,8,128]{2,1,0:T(8,128)S(1)} %broadcast_in_dim.83), channel_id=1, replica_groups=mesh['y'=8,'z'=8,'x'=4,'c'=2] {'y','x'}, dimensions={0} | all-to-all | bytes 262144 | tf_op jit(solution)/shard_map/all_to_all | solution.py:36
  77.7 11.8 %all_to_all.52 = f32[16,8,128]{2,1,0:T(8,128)S(1)} all-to-all(f32[16,8,128]{2,1,0:T(8,128)S(1)} %broadcast_in_dim.84), channel_id=1, replica_groups=mesh['y'=8,'z'=8,'x'=4,'c'=2] {'z','c'}, dimensions={0} | all-to-all | bytes 131072 | tf_op jit(solution)/shard_map/all_to_all | solution.py:36
  89.7 2.9 %cholesky.44 = f32[32,32]{1,0:T(8,128)S(1)} custom-call(f32[32,32]{1,0:T(8,128)S(1)} %fusion.24), custom_call_target="Cholesky" | custom-call | tf_op jit(solution)/shard_map/jit(cholesky)/cholesky | solution.py:26
  92.6 0.6 compare_reduce_fusion.1
  93.3 0.7 fusion.29
  93.9 2.4 %custom-call.8 = f32[1,32,32]{1,2,0:T(8,128)S(1)} custom-call(f32[1,32,32]{2,1,0:T(8,128)S(1)} %fusion.29), custom_call_target="InvertDiagBlocksLowerTriangular" | custom-call | tf_op jit(solution)/shard_map/jit(_solve_triangular)/triangular_solve | solution.py:28
  96.4 0.2 fusion.19
  96.6 0.6 fusion.53
  97.2 0.6 fusion.54
  97.8 0.7 broadcast_in_dim.86
  98.5 3.9 %all-to-all-start.5 = ((f32[32,8,128]{2,1,0:T(8,128)}), f32[32,8,128]{2,1,0:T(8,128)S(1)}, u32[]{:S(2)}, u32[]{:S(2)}) async-start(f32[32,8,128]{2,1,0:T(8,128)} %broadcast_in_dim.86), calls=%async_computation.5 | async-start | bytes 262144 | tf_op jit(solution)/shard_map/all_to_all | solution.py:36
  102.5 0.7 gather_fusion
  103.3 9.0 %all-to-all-done.5 = f32[32,8,128]{2,1,0:T(8,128)S(1)} async-done(((f32[32,8,128]{2,1,0:T(8,128)}), f32[32,8,128]{2,1,0:T(8,128)S(1)}, u32[]{:S(2)}, u32[]{:S(2)}) %all-to-all-start.5) | async-done | bytes 131104 | tf_op jit(solution)/shard_map/all_to_all | solution.py:36
  112.3 0.6 broadcast_in_dim.87
  113.0 4.9 %all-to-all-start.6 = ((f32[16,8,128]{2,1,0:T(8,128)}), f32[16,8,128]{2,1,0:T(8,128)S(1)}, u32[]{:S(2)}, u32[]{:S(2)}) async-start(f32[16,8,128]{2,1,0:T(8,128)} %broadcast_in_dim.87), calls=%async_computation.6 | async-start | bytes 131072 | tf_op jit(solution)/shard_map/all_to_all | solution.py:36
  117.8 0.5 fusion.40
  118.4 7.3 %all-to-all-done.6 = f32[16,8,128]{2,1,0:T(8,128)S(1)} async-done(((f32[16,8,128]{2,1,0:T(8,128)}), f32[16,8,128]{2,1,0:T(8,128)S(1)}, u32[]{:S(2)}, u32[]{:S(2)}) %all-to-all-start.6) | async-done | bytes 65568 | tf_op jit(solution)/shard_map/all_to_all | solution.py:36
  125.8 2.9 %cholesky.55 = f32[32,32]{1,0:T(8,128)S(1)} custom-call(f32[32,32]{1,0:T(8,128)S(1)} %fusion.22), custom_call_target="Cholesky" | custom-call | tf_op jit(solution)/shard_map/jit(cholesky)/cholesky | solution.py:26
  128.8 0.6 compare_reduce_fusion
  129.4 1.5 %fusion.30 = f32[32,32]{1,0:T(8,128)S(1)} fusion(f32[32,32]{1,0:T(8,128)S(1)} %cholesky.44, f32[32,32]{1,0:T(8,128)S(1)} %cholesky.55, pred[]{:T(512)} %compare_reduce_fusion, pred[]{:T(512)} %compare_reduce_fusion.1), kind=kOutput, calls=%fused_computation.61 | convolution fusion | flops 399360 | bytes 12290 | tf_op jit(solution)/shard_map/dot_general | solution.py:71
  130.9 0.7 select_bitcast_fusion
  131.6 2.4 %custom-call.9 = f32[1,32,32]{1,2,0:T(8,128)S(1)} custom-call(f32[1,32,32]{2,1,0:T(8,128)S(1)} %select_bitcast_fusion), custom_call_target="InvertDiagBlocksLowerTriangular" | custom-call | tf_op jit(solution)/shard_map/jit(_solve_triangular)/triangular_solve | solution.py:28
  134.0 0.2 fusion.17
  134.3 0.6 fusion.64
  134.9 0.9 select_reduce_fusion
  136.4 0.8 fusion.34
  137.3 0.8 fusion.14
  138.1 0.2 fusion.55
  138.3 0.2 fusion.13
  138.7 0.2 fusion.12
  138.9 0.2 fusion.57
  139.0 0.2 fusion.11
  139.6 0.2 fusion.59
  140.0 0.2 fusion.60
  140.2 0.2 fusion.8
  140.7 0.2 fusion.62
  141.1 0.2 fusion.63
  141.3 0.2 fusion.5
  141.5 0.3 fusion.32
  141.9 2.6 %convolution_multiply_fusion = f32[96,4096]{1,0:T(8,128)} fusion(f32[96,96]{1,0:T(8,128)S(1)} %fusion.32, f32[32,4096]{1,0:T(8,128)S(1)} %fusion.64, f32[64,4096]{1,0:T(8,128)S(1)} %copy-done), kind=kOutput, calls=%fused_computation.1 | convolution fusion | flops 453771264 | bytes 3182592 | tf_op jit(solution)/shard_map/dot_general | solution.py:78
  (44 shorter events, 2.7 us)
Async XLA Ops:
  0.6 20.9 %copy-start = (f32[64,4096]{1,0:T(8,128)S(1)}, f32[64,4096]{1,0:T(8,128)}, u32[]{:S(2)}) copy-start(f32[64,4096]{1,0:T(8,128)} %param.7) | copy-start | bytes 3145732
  0.6 19.8 %all-to-all-start = ((bf16[8,8,4096]{2,0,1:T(8,128)(2,1)}), bf16[8,8,4096]{2,0,1:T(8,128)(2,1)S(1)}, u32[]{:S(2)}, u32[]{:S(2)}) async-start(bf16[8,8,4096]{2,0,1:T(8,128)(2,1)} %bitcast.86), calls=%async_computation | async-start | bytes 1048576 | tf_op jit(solution)/shard_map/all_to_all | solution.py:50
  77.7 24.7 %copy-start.2 = (f32[64]{0:T(128)S(1)}, f32[64]{0:T(128)}, u32[]{:S(2)}) copy-start(f32[64]{0:T(128)} %param.8) | copy-start | bytes 772
  98.5 13.8 %all-to-all-start.5 = ((f32[32,8,128]{2,1,0:T(8,128)}), f32[32,8,128]{2,1,0:T(8,128)S(1)}, u32[]{:S(2)}, u32[]{:S(2)}) async-start(f32[32,8,128]{2,1,0:T(8,128)} %broadcast_in_dim.86), calls=%async_computation.5 | async-start | bytes 262144 | tf_op jit(solution)/shard_map/all_to_all | solution.py:36
  113.0 12.7 %all-to-all-start.6 = ((f32[16,8,128]{2,1,0:T(8,128)}), f32[16,8,128]{2,1,0:T(8,128)S(1)}, u32[]{:S(2)}, u32[]{:S(2)}) async-start(f32[16,8,128]{2,1,0:T(8,128)} %broadcast_in_dim.87), calls=%async_computation.6 | async-start | bytes 131072 | tf_op jit(solution)/shard_map/all_to_all | solution.py:36
  141.5 3.0 %copy-start.1 = (f32[96,96]{1,0:T(8,128)}, f32[96,96]{1,0:T(8,128)S(1)}, u32[]{:S(2)}) copy-start(f32[96,96]{1,0:T(8,128)S(1)} %fusion.5) | copy-start | bytes 110596

commit v2 on v1

v2 whole, which is shorter than its diff:
```python
import math

import jax
import jax.numpy as jnp
from jax import lax
from jax.experimental import pallas as pl
from jax.experimental.pallas import tpu as pltpu
from jax.sharding import Mesh, PartitionSpec as P

NEWTON = 10
HIGH = lax.Precision.HIGHEST
ALL = ("y", "z", "x", "c")
F32 = jnp.float32
BF16 = jnp.bfloat16
MODE_SLICES = 4
COLUMN_SLICES = 3
DENSE_SLICES = 5
CHUNK = 1024
PIECE = 512
INTERPRET = False


def iota(shape, axis):
    return lax.broadcasted_iota(jnp.int32, shape, axis)


def eye_mask(size):
    return iota((size, size), 0) == iota((size, size), 1)


def to_column(row):
    size = row.shape[1]
    return jnp.sum(jnp.where(eye_mask(size), row, 0.0), axis=1, keepdims=True)


def to_row(column):
    size = column.shape[0]
    return jnp.sum(jnp.where(eye_mask(size), column, 0.0), axis=0, keepdims=True)


def two_sum(a, b):
    total = a + b
    part = total - a
    return total, (a - (total - part)) + (b - part)


def split(a):
    scaled = a * 4097.0
    high = scaled - (scaled - a)
    return high, a - high


def two_product(a, b):
    product = a * b
    a_high, a_low = split(a)
    b_high, b_low = split(b)
    error = ((a_high * b_high - product) + a_high * b_low + a_low * b_high) + a_low * b_low
    return product, error


def power_of_two(bound):
    rest = bound
    scale = jnp.full_like(bound, 2.0)
    inverse = jnp.full_like(bound, 0.5)
    for step in (64, 32, 16, 8, 4, 2, 1):
        up, down = float(2.0**step), float(2.0**-step)
        large = rest >= up
        rest = jnp.where(large, rest * down, rest)
        scale = jnp.where(large, scale * up, scale)
        inverse = jnp.where(large, inverse * down, inverse)
    for step in (32, 16, 8, 4, 2, 1):
        up, down = float(2.0**step), float(2.0**-step)
        small = rest < 2.0 * down
        rest = jnp.where(small, rest * up, rest)
        scale = jnp.where(small, scale * down, scale)
        inverse = jnp.where(small, inverse * up, inverse)
    return scale, inverse


def slices_of(high, low, inverse, count):
    rest = high * (inverse * 128.0)
    out = []
    for index in range(count):
        if index == 2 and low is not None:
            rest = rest + low * (inverse * (128.0 * 65536.0))
        whole = jnp.round(rest)
        out.append(whole)
        if index + 1 < count:
            rest = (rest - whole) * 256.0
    return out


def dot_nt(a, b):
    return lax.dot_general(a, b, (((1,), (1,)), ((), ())), preferred_element_type=F32)


def levels_of(products, size, level_count):
    out = []
    for level in range(level_count):
        total = None
        for j, product in enumerate(products):
            i = level - j
            if 0 <= i and (i + 1) * size <= product.shape[0]:
                block = product[i * size : (i + 1) * size]
                total = block if total is None else total + block
        out.append(total)
    return out


def combine(leading, rest):
    high, low = leading[0], None
    for part in leading[1:]:
        high, error = two_sum(high, part)
        low = error if low is None else low + error
    tail = None
    for level in reversed(rest):
        tail = level if tail is None else level + tail * (1.0 / 256.0)
    tail = tail * (1.0 / 256.0)
    low = tail if low is None else low + tail
    return two_sum(high, low)


def long_gram(left_ref, left_size, right_ref, right_size, right_count, level_count):
    left_count = left_ref.shape[0] // left_size
    leading, rest = [], None
    for start in range(0, left_ref.shape[1], CHUNK):
        products = []
        for j in range(right_count):
            rows = min(left_count, level_count - j) * left_size
            products.append(
                dot_nt(
                    left_ref[0:rows, start : start + CHUNK],
                    right_ref[j * right_size : (j + 1) * right_size, start : start + CHUNK],
                )
            )
        levels = levels_of(products, left_size, level_count)
        leading.append(levels[0])
        rest = levels[1:] if rest is None else [a + b for a, b in zip(rest, levels[1:])]
    return combine(leading, rest)


def modes_kernel(basis_ref, parts_ref, scale_ref, pair_ref, gram_ref):
    size, lanes = basis_ref.shape
    bound = jnp.zeros((size, 1), F32)
    for start in range(0, lanes, CHUNK):
        bound = jnp.maximum(bound, jnp.max(jnp.abs(basis_ref[:, start : start + CHUNK]), axis=1, keepdims=True))
    scale, inverse = power_of_two(bound)
    scale_ref[...] = scale
    for start in range(0, lanes, PIECE):
        block = basis_ref[:, start : start + PIECE]
        for index, part in enumerate(slices_of(block, None, inverse, MODE_SLICES)):
            parts_ref[index * size : (index + 1) * size, start : start + PIECE] = part.astype(BF16)
        rounded = block.astype(BF16)
        pair_ref[0:size, start : start + PIECE] = rounded
        pair_ref[size : 2 * size, start : start + PIECE] = (block - rounded.astype(F32)).astype(BF16)
    high, low = long_gram(parts_ref, size, parts_ref, size, MODE_SLICES, MODE_SLICES)
    factor = scale * (1.0 / 16384.0)
    across = to_row(scale)
    gram_ref[0] = high * factor * across
    gram_ref[1] = low * factor * across


def columns_kernel(ids_ref, archive_ref, parts_ref, scale_ref, gram_ref, columns_ref, packed_ref, slices):
    count = ids_ref.shape[0]
    total, lanes = archive_ref.shape
    modes = scale_ref.shape[0]
    picker = jnp.where(ids_ref[...] == iota((count, total), 1), 1.0, 0.0).astype(BF16)
    bound = jnp.zeros((count, 1), F32)
    for start in range(0, lanes, PIECE):
        block = jnp.dot(picker, archive_ref[:, start : start + PIECE], preferred_element_type=F32)
        columns_ref[:, start : start + PIECE] = block.astype(BF16)
        bound = jnp.maximum(bound, jnp.max(jnp.abs(block), axis=1, keepdims=True))
    scale, inverse = power_of_two(bound)
    for start in range(0, lanes, PIECE):
        block = columns_ref[:, start : start + PIECE].astype(F32)
        for index, part in enumerate(slices_of(block, None, inverse, COLUMN_SLICES)):
            slices[index * count : (index + 1) * count, start : start + PIECE] = part.astype(BF16)
    across = to_row(scale)
    p_high, p_low = long_gram(parts_ref, modes, slices, count, COLUMN_SLICES, 4)
    factor = scale_ref[...] * (1.0 / 16384.0)
    p_high, p_low = p_high * factor * across, p_low * factor * across
    c_high, c_low = long_gram(slices, count, slices, count, COLUMN_SLICES, 4)
    factor = scale * (1.0 / 16384.0)
    c_high, c_low = c_high * factor * across, c_low * factor * across
    g_high, g_low = gram_ref[0], gram_ref[1]
    n = count
    packed_ref[0:n, :] = jnp.concatenate([p_high[0:n], p_low[0:n], p_high[n:], p_low[n:]], axis=1)
    packed_ref[n : 2 * n, :] = jnp.concatenate([c_high, c_low, g_high[0:n, 0:n], g_low[0:n, 0:n]], axis=1)
    packed_ref[2 * n :, :] = jnp.concatenate(
        [g_high[n:, 0:n], g_low[n:, 0:n], g_high[n:, n:], g_low[n:, n:]], axis=1
    )


def sum_pairs(load, count):
    high = load(0)
    error = jnp.zeros_like(high)
    for index in range(1, count):
        high, part = two_sum(high, load(index))
        error = error + part
    odd = (iota(high.shape, 1) // 32) % 2 == 1
    return jnp.where(odd, high + pltpu.roll(error, 32, 1), high)


def half_kernel(place_ref, both_ref, out_ref):
    copies, rows, _ = out_ref.shape
    start = pl.multiple_of(place_ref[0] * rows, 8)
    total = sum_pairs(lambda index: both_ref[index, pl.ds(start, rows), :], both_ref.shape[0])
    for index in range(copies):
        out_ref[index] = total


def sum_kernel(parts_ref, out_ref):
    total = sum_pairs(lambda index: parts_ref[index], parts_ref.shape[0])
    if len(out_ref.shape) == 2:
        out_ref[...] = total
    else:
        for index in range(out_ref.shape[0]):
            out_ref[index] = total


def high_dot(a, b):
    return jnp.dot(a, b, precision=HIGH, preferred_element_type=F32)


def slice_product(left, right, level_count):
    size = left[0].shape[0]
    stacked = jnp.concatenate(left, axis=0).astype(BF16)
    products = []
    for j, part in enumerate(right):
        rows = (level_count - j) * size
        products.append(jnp.dot(stacked[0:rows], part.astype(BF16), preferred_element_type=F32))
    levels = levels_of(products, size, level_count)
    return combine(levels[0:1], levels[1:])


def triangle(high, low):
    size = high.shape[0]
    rows = iota((size, size), 0)
    for j in range(size - 1):
        row_high, row_low = high[j : j + 1, :], low[j : j + 1, :]
        below = iota((size, 1), 0) > j
        col_high = jnp.where(below, high[:, j : j + 1], 0.0)
        col_low = jnp.where(below, low[:, j : j + 1], 0.0)
        d_high, d_low = row_high[:, j : j + 1], row_low[:, j : j + 1]
        q_high = 1.0 / d_high
        p_high, p_low = two_product(d_high, q_high)
        q_low = q_high * (((1.0 - p_high) - p_low) - d_low * q_high)
        w_high, w_error = two_product(col_high, q_high)
        w_low = w_error + (col_high * q_low + col_low * q_high)
        u_high, u_error = two_product(w_high, row_high)
        u_low = u_error + (w_high * row_low + w_low * row_high)
        s_high, s_error = two_sum(high, -u_high)
        s_low = s_error + (low - u_low)
        high = s_high + s_low
        low = s_low - (high - s_high)
    pivots = jnp.sum(jnp.where(eye_mask(size), high, 0.0), axis=1, keepdims=True)
    return jnp.where(iota((size, size), 1) >= rows, high * lax.rsqrt(pivots), 0.0)


def dense(packed, values, total_rows):
    n = packed.shape[0] // 3
    m = 2 * n
    width = m + n
    square_scale = 1.0 / total_rows
    scale = math.sqrt(square_scale)

    def block(row, lane):
        return packed[row * n : (row + 1) * n, lane * n : (lane + 1) * n]

    p_high = jnp.concatenate([block(0, 0), block(0, 2)], axis=0)
    p_low = jnp.concatenate([block(0, 1), block(0, 3)], axis=0)
    p_high, p_low = two_sum(p_high, p_low)
    c_high, c_low = two_sum(block(1, 0), block(1, 1))
    g_high = jnp.concatenate(
        [
            jnp.concatenate([block(1, 2), block(2, 0).T], axis=1),
            jnp.concatenate([block(2, 0), block(2, 2)], axis=1),
        ],
        axis=0,
    )
    g_low = jnp.concatenate(
        [
            jnp.concatenate([block(1, 3), block(2, 1).T], axis=1),
            jnp.concatenate([block(2, 1), block(2, 3)], axis=1),
        ],
        axis=0,
    )
    eye_m = jnp.where(eye_mask(m), 1.0, 0.0)
    t_high, t_error = two_sum(2.0 * eye_m, -g_high)
    t_high, t_low = two_sum(t_high, t_error - g_low)

    t_scale, t_inverse = power_of_two(jnp.max(jnp.max(jnp.abs(t_high), axis=1, keepdims=True), axis=0, keepdims=True))
    p_scale, p_inverse = power_of_two(jnp.max(jnp.abs(p_high), axis=0, keepdims=True))
    p_slices = slices_of(p_high, p_low, p_inverse, DENSE_SLICES)
    h_high, h_low = slice_product(slices_of(t_high, t_low, t_inverse, DENSE_SLICES), p_slices, DENSE_SLICES)
    h_scale, h_inverse = power_of_two(jnp.max(jnp.abs(h_high), axis=0, keepdims=True))
    pt_slices = [part.T for part in p_slices]
    q_high, q_low = slice_product(pt_slices, slices_of(h_high, h_low, h_inverse, DENSE_SLICES), DENSE_SLICES)
    factor = to_column(p_scale) * (1.0 / 16384.0)
    across = h_scale * (p_scale * (t_scale * (1.0 / 16384.0)))
    q_high, q_low = q_high * factor * across, q_low * factor * across
    r_high, r_error = two_sum(c_high, -q_high)
    one_high, one_low = two_sum(r_high, r_error + (c_low - q_low))

    eye_n = eye_mask(n)
    own = jnp.sum(jnp.where(eye_n, one_high, 0.0), axis=0, keepdims=True)
    energy = jnp.sum(jnp.where(eye_n, c_high, 0.0), axis=0, keepdims=True)
    novelty = own / energy

    values_column = to_column(values)
    projection = p_high * scale
    gram = one_high * square_scale
    turned = projection.T
    mixed = projection * values_column
    kernel_top = jnp.concatenate([eye_m * (values_column * values_column), mixed], axis=1)
    kernel_low = jnp.concatenate([mixed.T, high_dot(turned, projection) + gram], axis=1)
    inner = jnp.concatenate([kernel_top, kernel_low], axis=0)
    eye_w = jnp.where(eye_mask(width), 1.0, 0.0)
    total = jnp.sum(jnp.sum(inner * eye_w, axis=1, keepdims=True), axis=0, keepdims=True)
    shifted = (inner - (total / width) * eye_w) / total
    slope = eye_w
    origin = -1.0 / width
    for _ in range(NEWTON):
        squared = high_dot(shifted, shifted)
        divided = (origin * origin) * eye_w + origin * shifted + squared
        slope = 1.5 * slope - 0.5 * high_dot(slope, divided)
        shifted = 1.5 * shifted - 0.5 * high_dot(shifted, squared)
        origin = 1.5 * origin - 0.5 * origin * origin * origin
    blend = 0.5 * (eye_w + shifted)
    slope = slope * (0.5 / total)

    upper = triangle(one_high, one_low) * scale
    core = jnp.concatenate(
        [
            jnp.concatenate([eye_m * values_column, projection], axis=1),
            jnp.concatenate([jnp.zeros((n, m), F32), upper], axis=1),
        ],
        axis=0,
    )
    half = high_dot(core, slope)
    projector = (0.5 * (1.0 + origin)) * eye_w + lax.dot_general(
        half, core, (((1,), (1,)), ((), ())), precision=HIGH, preferred_element_type=F32
    )
    weights = jnp.concatenate([blend[:, 0:m] * (values * math.sqrt(total_rows)), blend[:, m:]], axis=1)
    return weights, projector, novelty


def finish_kernel(total_rows, packed_ref, values_ref, pair_ref, columns_ref, filtered_ref, projector_ref, novelty_ref, left):
    modes = values_ref.shape[1]

    @pl.when(pl.program_id(0) == 0)
    def _():
        weights, projector, novelty = dense(packed_ref[...], values_ref[...], total_rows)
        projector_ref[...] = projector
        novelty_ref[...] = novelty
        rounded = weights.astype(BF16)
        rest = (weights - rounded.astype(F32)).astype(BF16)
        left[...] = jnp.concatenate(
            [rounded[:, 0:modes], rounded[:, 0:modes], rest[:, 0:modes], rounded[:, modes:], rest[:, modes:]], axis=1
        )

    lanes = filtered_ref.shape[1]
    for start in range(0, lanes, 256):
        where = slice(start, start + 256)
        first, second, third = pair_ref[0:modes, where], pair_ref[modes:, where], columns_ref[:, where]
        right = jnp.concatenate([first, second, first, third, third], axis=0)
        filtered_ref[:, where] = jnp.dot(left[...], right, preferred_element_type=F32)


def vmem(count):
    return [pl.BlockSpec(memory_space=pltpu.VMEM)] * count


def shape(dims, dtype=F32):
    return jax.ShapeDtypeStruct(dims, dtype)


def prepare(basis):
    modes, lanes = basis.shape
    return pl.pallas_call(
        modes_kernel,
        out_shape=(
            shape((MODE_SLICES * modes, lanes), BF16),
            shape((modes, 1)),
            shape((2 * modes, lanes), BF16),
            shape((2, modes, modes)),
        ),
        in_specs=vmem(1),
        out_specs=tuple(vmem(4)),
        interpret=INTERPRET,
        name="modes",
    )(basis)


def gather(ids, everything, parts, scale, gram):
    count, lanes = ids.shape[0], everything.shape[1]
    return pl.pallas_call(
        columns_kernel,
        out_shape=(shape((count, lanes), BF16), shape((3 * count, 128))),
        in_specs=vmem(5),
        out_specs=tuple(vmem(2)),
        scratch_shapes=[pltpu.VMEM((COLUMN_SLICES * count, lanes), BF16)],
        interpret=INTERPRET,
        name="columns",
    )(ids, everything, parts, scale, gram)


def take_half(place, both, copies):
    rows = both.shape[1] // 2
    return pl.pallas_call(
        half_kernel,
        out_shape=shape((copies, rows, 128)),
        in_specs=[pl.BlockSpec(memory_space=pltpu.SMEM)] + vmem(1),
        out_specs=vmem(1)[0],
        interpret=INTERPRET,
        name="half",
    )(place, both)


def add_up(parts, copies):
    rows = parts.shape[1]
    return pl.pallas_call(
        sum_kernel,
        out_shape=shape((rows, 128) if copies is None else (copies, rows, 128)),
        in_specs=vmem(1),
        out_specs=vmem(1)[0],
        interpret=INTERPRET,
        name="add",
    )(parts)


def finish(total_rows, packed, values, pair, columns):
    import functools

    modes, count, lanes = values.shape[1], columns.shape[0], columns.shape[1]
    width = modes + count
    steps = 4
    return pl.pallas_call(
        functools.partial(finish_kernel, total_rows),
        grid=(steps,),
        out_shape=(shape((width, lanes)), shape((width, width)), shape((1, count))),
        in_specs=[
            pl.BlockSpec((3 * count, 128), lambda i: (0, 0)),
            pl.BlockSpec((1, modes), lambda i: (0, 0)),
            pl.BlockSpec((2 * modes, lanes // steps), lambda i: (0, i)),
            pl.BlockSpec((count, lanes // steps), lambda i: (0, i)),
        ],
        out_specs=(
            pl.BlockSpec((width, lanes // steps), lambda i: (0, i)),
            pl.BlockSpec((width, width), lambda i: (0, 0)),
            pl.BlockSpec((1, count), lambda i: (0, 0)),
        ),
        scratch_shapes=[pltpu.VMEM((width, 256), BF16)],
        interpret=INTERPRET,
        name="finish",
    )(packed, values, pair, columns)


def exchange(copies, axes):
    return lax.all_to_all(copies, axes, 0, 0, tiled=True)


def per_device(basis, values, archive, window_ids):
    total_rows = basis.shape[1]
    for name in ALL:
        total_rows *= lax.axis_size(name)
    everything = lax.all_to_all(archive, ("x", "c"), split_axis=1, concat_axis=0, tiled=True)
    parts, scale, pair, gram = prepare(basis)
    columns, packed = gather(window_ids[:, None], everything, parts, scale, gram)
    both = lax.all_gather(packed, "c")
    plane = lax.axis_size("y") * lax.axis_size("x")
    place = lax.axis_index("c").astype(jnp.int32)[None]
    first = exchange(take_half(place, both, plane), ("y", "x"))
    second = exchange(add_up(first, lax.axis_size("z")), ("z",))
    packed = lax.all_gather(add_up(second, None), "c", tiled=True)
    filtered, projector, novelty = finish(total_rows, packed, values[None, :], pair, columns)
    return (filtered, projector, novelty.reshape(-1))


def solution(mesh):
    fine = Mesh(mesh.devices.reshape(8, 8, 4, 2), ALL)
    placed = (P(None, ALL), P(), P(("x", "c"), ("y", "z")), P())
    return jax.shard_map(
        per_device,
        mesh=fine,
        in_specs=placed,
        out_specs=(P(None, ALL), P(), P()),
        check_vma=False,
    )
```

time: 145 us -> 96.4 us (0.66)
  Pallas kernels: 0 us -> 24.1 us
  waiting for transfers between devices: 25.6 us -> 4.75 us
  matrix products: 15.7 us -> 0 us
  other arithmetic: 14.3 us -> 0 us
  blocking collectives: 65.2 us -> 54.4 us
  starting transfers between devices: 19.1 us -> 10.2 us
  local copies, waits for them, and re-layouts: 3.03 us -> 1.48 us
    pallas_call x0 -> x6, Pallas kernels: none -> 24.1 us  [the longest x1 9.66 us: finish(): pl.pallas_call(functools.partial(finish_kernel, total_rows), grid=(steps,...]
    all_to_all x4 -> x2, blocking collectives: 65.2 us -> 43.9 us  [exchange(): return lax.all_to_all(copies, axes, 0, 0, tiled=True)]
    all_to_all x2 -> x0, waiting for transfers between devices: 16.3 us -> none  [sum_over(): return jnp.sum(lax.all_to_all(copies, axes, 0, 0, tiled=True), axis=0)]
    dot_general x31 -> x0, matrix products: 15.2 us -> none  [the longest x1 2.62 us: per_device(): filtered = jnp.dot(weights, stacked, precision=HIGH) * math.sqrt(total_rows)]
    another operation x10 -> x0, other arithmetic: 13.4 us -> none  [the longest x6 7.19 us: inverse_lower(): factor = jnp.linalg.cholesky(gram)]
    all_gather x0 -> x2, blocking collectives: none -> 10.5 us  [the longest x1 6.4 us: per_device(): packed = lax.all_gather(add_up(second, None), 'c', tiled=True)]
    all_to_all x2 -> x0, starting transfers between devices: 8.75 us -> none  [sum_over(): return jnp.sum(lax.all_to_all(copies, axes, 0, 0, tiled=True), axis=0)]
    all_to_all x1, waiting for transfers between devices: 9.3 us -> 4.75 us  [per_device(): lax.all_to_all(archive, ('x', 'c'), split_axis=1, concat_axis=0, tiled=True)]
  transfers between devices with their start and end apart: 3 -> 1, of which waited for: 3 -> 1; matrix products, arithmetic and copies ran while one was open for 1% -> 1% of each run, Pallas kernels for 0% -> 4%
where the time goes in v2:
time: 96.4 us; the launch traced here: 95.6 us
  blocking collectives  54.4 us (56%)
  Pallas kernels  24.1 us (25%)
  starting transfers between devices  10.2 us (11%)
  waiting for transfers between devices  4.75 us (5%)
  local copies, waits for them, and re-layouts  1.48 us (2%)
    all_to_all x2, blocking collectives, exchange(): return lax.all_to_all(copies, axes, 0, 0, tiled=True)  43.9 us
    all_to_all x1, starting transfers between devices, per_device(): lax.all_to_all(archive, ('x', 'c'), split_axis=1, concat_axis=0, tiled=True)  10.2 us
    pallas_call x1, Pallas kernels, finish(): pl.pallas_call(functools.partial(finish_kernel, total_rows), grid=(steps,...  9.66 us
    all_gather x1, blocking collectives, per_device(): packed = lax.all_gather(add_up(second, None), 'c', tiled=True)  6.4 us
    pallas_call x1, Pallas kernels, gather(): pl.pallas_call(columns_kernel, out_shape=(shape((count, lanes), BF16), sh...  4.88 us
    all_to_all x1, waiting for transfers between devices, per_device(): lax.all_to_all(archive, ('x', 'c'), split_axis=1, concat_axis=0, tiled=True)  4.75 us
    all_gather x1, blocking collectives, per_device(): both = lax.all_gather(packed, 'c')  4.08 us
    pallas_call x1, Pallas kernels, prepare(): pl.pallas_call(modes_kernel, out_shape=(shape((MODE_SLICES * modes, lanes...  3.94 us
  transfers between devices with their start and end apart: 1, of which 1 were waited for; matrix products, arithmetic and copies ran while one was open for 1% of the time, Pallas kernels for 4%

profile of v2, /device:TPU:1, one launch (start us, length us, event | category | flops | bytes accessed | tf_op | source)
XLA Modules:
  0.0 95.6 jit_solution(13333778112517388171)
XLA Ops:
  0.6 0.0 copy-start.1
  0.6 10.2 %all-to-all-start = ((bf16[8,8,4096]{2,0,1:T(8,128)(2,1)}), bf16[8,8,4096]{2,0,1:T(8,128)(2,1)S(1)}, u32[]{:S(2)}, u32[]{:S(2)}) async-start(bf16[8,8,4096]{2,0,1:T(8,128)(2,1)} %bitcast.10), calls=%async_computation | async-start | bytes 1048576 | tf_op jit(solution)/shard_map/all_to_all | solution.py:467
  10.9 3.9 %modes.1 = (bf16[256,4096]{1,0:T(8,128)(2,1)}, f32[64,1]{1,0:T(8,128)}, bf16[128,4096]{1,0:T(8,128)(2,1)}, f32[2,64,64]{2,1,0:T(8,128)}) custom-call(f32[64,4096]{1,0:T(8,128)} %basis_ref.1), custom_call_target="tpu_custom_call" | custom-call | tf_op jit(solution)/shard_map/modes/pallas_call | solution.py:380
  14.8 0.0 copy-done.1
  14.8 0.7 copy.7.ids_ref
  15.5 4.8 %all-to-all-done = bf16[8,8,4096]{2,0,1:T(8,128)(2,1)S(1)} async-done(((bf16[8,8,4096]{2,0,1:T(8,128)(2,1)}), bf16[8,8,4096]{2,0,1:T(8,128)(2,1)S(1)}, u32[]{:S(2)}, u32[]{:S(2)}) %all-to-all-start) | async-done | bytes 524320 | tf_op jit(solution)/shard_map/all_to_all | solution.py:467
  20.3 0.0 copy-start
  20.3 0.8 copy-done
  21.1 4.9 %columns.1 = (bf16[32,4096]{1,0:T(8,128)(2,1)}, f32[96,128]{1,0:T(8,128)}) custom-call(s32[32,1]{1,0:T(8,128)} %copy.7.ids_ref, bf16[64,4096]{1,0:T(8,128)(2,1)} %bitcast.9, bf16[256,4096]{1,0:T(8,128)(2,1)} %get-tuple-element.12.parts_ref, f32[64,1]{1,0:T(8,128)} %get-tuple-element.13.scale_ref, f32[2,64,64]{2,1,0:T(8,128)} %get-tuple-element.14.gram_ref), custom_call_target="tpu_custom_call" | custom-call | tf_op jit(solution)/shard_map/columns/pallas_call | solution.py:397
  25.9 4.1 %all-gather = f32[192,128]{1,0:T(8,128)} all-gather(f32[96,128]{1,0:T(8,128)} %get-tuple-element.15), channel_id=2, replica_groups=mesh['y'=8,'z'=8,'x'=4,'c'=2] {'c'}, dimensions={0}, use_global_device_ids=true | all-gather | bytes 147456 | tf_op jit(solution)/shard_map/all_gather | solution.py:470
  30.0 1.9 %half.1 = f32[32,48,128]{2,1,0:T(8,128)} custom-call(s32[1]{0:T(128)} %bitcast.place_ref, f32[2,96,128]{2,1,0:T(8,128)} %bitcast.11), custom_call_target="tpu_custom_call" | custom-call | tf_op jit(solution)/shard_map/half/pallas_call | solution.py:410
  31.9 26.8 %all_to_all.29.parts_ref = f32[32,48,128]{2,1,0:T(8,128)} all-to-all(f32[32,48,128]{2,1,0:T(8,128)} %half.1), channel_id=1, replica_groups=mesh['y'=8,'z'=8,'x'=4,'c'=2] {'y','x'}, dimensions={0} | all-to-all | bytes 1572864 | tf_op jit(solution)/shard_map/all_to_all | solution.py:460
  58.8 2.1 %add.2 = f32[8,48,128]{2,1,0:T(8,128)} custom-call(f32[32,48,128]{2,1,0:T(8,128)} %all_to_all.29.parts_ref), custom_call_target="tpu_custom_call" | custom-call | tf_op jit(solution)/shard_map/add/pallas_call | solution.py:422
  60.8 17.1 %all_to_all.30.parts_ref = f32[8,48,128]{2,1,0:T(8,128)} all-to-all(f32[8,48,128]{2,1,0:T(8,128)} %add.2), channel_id=1, replica_groups=mesh['y'=8,'z'=8,'x'=4,'c'=2] {'z'}, dimensions={0} | all-to-all | bytes 393216 | tf_op jit(solution)/shard_map/all_to_all | solution.py:460
  77.9 1.6 %add.3 = f32[48,128]{1,0:T(8,128)} custom-call(f32[8,48,128]{2,1,0:T(8,128)} %all_to_all.30.parts_ref), custom_call_target="tpu_custom_call" | custom-call | tf_op jit(solution)/shard_map/add/pallas_call | solution.py:422
  79.6 6.4 %all_gather.11.packed_ref = f32[96,128]{1,0:T(8,128)} all-gather(f32[48,128]{1,0:T(8,128)} %add.3), channel_id=1, replica_groups=mesh['y'=8,'z'=8,'x'=4,'c'=2] {'c'}, dimensions={0}, use_global_device_ids=true | all-gather | bytes 73728 | tf_op jit(solution)/shard_map/all_gather | solution.py:475
  86.0 9.7 %finish.1 = (f32[96,4096]{1,0:T(8,128)}, f32[96,96]{1,0:T(8,128)}, f32[1,32]{1,0:T(1,128)}) custom-call(f32[96,128]{1,0:T(8,128)} %all_gather.11.packed_ref, f32[1,64]{1,0:T(1,128)} %bitcast.12, bf16[128,4096]{1,0:T(8,128)(2,1)} %get-tuple-element.16.pair_ref, bf16[32,4096]{1,0:T(8,128)(2,1)} %get-tuple-element.17.columns_ref), custom_call_target="tpu_custom_call" | custom-call | tf_op jit(solution)/shard_map/finish/pallas_call | solution.py:438
Async XLA Ops:
  0.6 14.2 %copy-start.1 = (s32[32]{0:T(128)S(1)}, s32[32]{0:T(128)}, u32[]{:S(2)}) copy-start(s32[32]{0:T(128)} %param.7) | copy-start | bytes 388
  0.6 19.6 %all-to-all-start = ((bf16[8,8,4096]{2,0,1:T(8,128)(2,1)}), bf16[8,8,4096]{2,0,1:T(8,128)(2,1)S(1)}, u32[]{:S(2)}, u32[]{:S(2)}) async-start(bf16[8,8,4096]{2,0,1:T(8,128)(2,1)} %bitcast.10), calls=%async_computation | async-start | bytes 1048576 | tf_op jit(solution)/shard_map/all_to_all | solution.py:467
  20.3 0.8 copy-start

commit v3 on v2

--- a/solution.py
+++ b/solution.py
@@ -1,3 +1,4 @@
+import functools
 import math
 
 import jax
@@ -139,7 +140,7 @@
     return combine(leading, rest)
 
 
-def modes_kernel(basis_ref, parts_ref, scale_ref, pair_ref, gram_ref):
+def modes_kernel(share, basis_ref, parts_ref, scale_ref, pair_ref, gram_ref):
     size, lanes = basis_ref.shape
     bound = jnp.zeros((size, 1), F32)
     for start in range(0, lanes, CHUNK):
@@ -156,14 +157,29 @@
     high, low = long_gram(parts_ref, size, parts_ref, size, MODE_SLICES, MODE_SLICES)
     factor = scale * (1.0 / 16384.0)
     across = to_row(scale)
-    gram_ref[0] = high * factor * across
-    gram_ref[1] = low * factor * across
-
-
-def columns_kernel(ids_ref, archive_ref, parts_ref, scale_ref, gram_ref, columns_ref, packed_ref, slices):
+    gram_ref[...] = (high * factor * across - jnp.where(eye_mask(size), share, 0.0)) + low * factor * across
+
+
+def cyclic(size):
+    rows, lanes = iota((size, size), 0), iota((size, size), 1)
+    return (lanes == rows + 1) | ((rows == size - 1) & (lanes == 0))
+
+
+def columns_kernel(
+    ids_ref, archive_ref, parts_hbm, scale_ref, gram_ref, columns_ref, packed_ref, slices, parts, arrived
+):
     count = ids_ref.shape[0]
     total, lanes = archive_ref.shape
     modes = scale_ref.shape[0]
+    starts = range(0, lanes, CHUNK)
+    copies = [
+        pltpu.make_async_copy(
+            parts_hbm.at[:, pl.ds(start, CHUNK)], parts.at[:, pl.ds(start, CHUNK)], arrived.at[index]
+        )
+        for index, start in enumerate(starts)
+    ]
+    for copy in copies:
+        copy.start()
     picker = jnp.where(ids_ref[...] == iota((count, total), 1), 1.0, 0.0).astype(BF16)
     bound = jnp.zeros((count, 1), F32)
     for start in range(0, lanes, PIECE):
@@ -175,47 +191,58 @@
         block = columns_ref[:, start : start + PIECE].astype(F32)
         for index, part in enumerate(slices_of(block, None, inverse, COLUMN_SLICES)):
             slices[index * count : (index + 1) * count, start : start + PIECE] = part.astype(BF16)
+
+    whole, lead_p, lead_c = None, [], []
+    height = MODE_SLICES * modes
+    for start, copy in zip(starts, copies):
+        copy.wait()
+        right = slices[:, start : start + CHUNK]
+        product = dot_nt(jnp.concatenate([parts[:, start : start + CHUNK], right], axis=0), right)
+        lead_p.append(product[0:modes, 0:count])
+        lead_c.append(product[height : height + count, 0:count])
+        whole = product if whole is None else whole + product
+    by_slice = [whole[:, j * count : (j + 1) * count] for j in range(COLUMN_SLICES)]
+    last = MODE_SLICES + COLUMN_SLICES - 2
+    p_high, p_low = combine(lead_p, levels_of([part[0:height] for part in by_slice], modes, last)[1:])
+    last = 2 * COLUMN_SLICES - 1
+    c_high, c_low = combine(lead_c, levels_of([part[height:] for part in by_slice], count, last)[1:])
     across = to_row(scale)
-    p_high, p_low = long_gram(parts_ref, modes, slices, count, COLUMN_SLICES, 4)
     factor = scale_ref[...] * (1.0 / 16384.0)
     p_high, p_low = p_high * factor * across, p_low * factor * across
-    c_high, c_low = long_gram(slices, count, slices, count, COLUMN_SLICES, 4)
     factor = scale * (1.0 / 16384.0)
     c_high, c_low = c_high * factor * across, c_low * factor * across
-    g_high, g_low = gram_ref[0], gram_ref[1]
     n = count
-    packed_ref[0:n, :] = jnp.concatenate([p_high[0:n], p_low[0:n], p_high[n:], p_low[n:]], axis=1)
-    packed_ref[n : 2 * n, :] = jnp.concatenate([c_high, c_low, g_high[0:n, 0:n], g_low[0:n, 0:n]], axis=1)
-    packed_ref[2 * n :, :] = jnp.concatenate(
-        [g_high[n:, 0:n], g_low[n:, 0:n], g_high[n:, n:], g_low[n:, n:]], axis=1
-    )
-
-
-def sum_pairs(load, count):
-    high = load(0)
+    gram = gram_ref[...]
+    last_block = gram[n:, n:]
+    last_diagonal = jnp.sum(jnp.where(eye_mask(n), last_block, 0.0), axis=1, keepdims=True)
+    c_low = jnp.where(cyclic(n), last_diagonal, c_low)
+    corner = jnp.where(iota((n, n), 0) >= iota((n, n), 1), gram[0:n, 0:n], last_block)
+    top = jnp.concatenate([p_high[0:n], p_low[0:n], p_high[n:], p_low[n:]], axis=1)
+    low = jnp.concatenate([c_high, c_low, gram[n:, 0:n], corner], axis=1)
+    for index in range(packed_ref.shape[0]):
+        packed_ref[index, 0:n, :] = top
+        packed_ref[index, n:, :] = low
+
+
+def sum_pairs(parts_ref):
+    high = parts_ref[0]
     error = jnp.zeros_like(high)
-    for index in range(1, count):
-        high, part = two_sum(high, load(index))
+    for index in range(1, parts_ref.shape[0]):
+        high, part = two_sum(high, parts_ref[index])
         error = error + part
-    odd = (iota(high.shape, 1) // 32) % 2 == 1
-    return jnp.where(odd, high + pltpu.roll(error, 32, 1), high)
-
-
-def half_kernel(place_ref, both_ref, out_ref):
-    copies, rows, _ = out_ref.shape
-    start = pl.multiple_of(place_ref[0] * rows, 8)
-    total = sum_pairs(lambda index: both_ref[index, pl.ds(start, rows), :], both_ref.shape[0])
-    for index in range(copies):
+    n = high.shape[0] // 2
+    rows, lanes = iota(high.shape, 0), iota(high.shape, 1)
+    top_takes = (rows < n) & ((lanes // n) % 2 == 1)
+    row, lane = rows - n, lanes - n
+    special = (lane == row + 1) | ((row == n - 1) & (lane == 0))
+    takes = top_takes | ((row >= 0) & (lane >= 0) & (lane < n) & jnp.logical_not(special))
+    return jnp.where(takes, high + pltpu.roll(error, n, 1), high)
+
+
+def sum_kernel(parts_ref, out_ref):
+    total = sum_pairs(parts_ref)
+    for index in range(out_ref.shape[0]):
         out_ref[index] = total
-
-
-def sum_kernel(parts_ref, out_ref):
-    total = sum_pairs(lambda index: parts_ref[index], parts_ref.shape[0])
-    if len(out_ref.shape) == 2:
-        out_ref[...] = total
-    else:
-        for index in range(out_ref.shape[0]):
-            out_ref[index] = total
 
 
 def high_dot(a, b):
@@ -258,7 +285,7 @@
 
 
 def dense(packed, values, total_rows):
-    n = packed.shape[0] // 3
+    n = packed.shape[0] // 2
     m = 2 * n
     width = m + n
     square_scale = 1.0 / total_rows
@@ -270,24 +297,19 @@
     p_high = jnp.concatenate([block(0, 0), block(0, 2)], axis=0)
     p_low = jnp.concatenate([block(0, 1), block(0, 3)], axis=0)
     p_high, p_low = two_sum(p_high, p_low)
-    c_high, c_low = two_sum(block(1, 0), block(1, 1))
-    g_high = jnp.concatenate(
-        [
-            jnp.concatenate([block(1, 2), block(2, 0).T], axis=1),
-            jnp.concatenate([block(2, 0), block(2, 2)], axis=1),
-        ],
-        axis=0,
-    )
-    g_low = jnp.concatenate(
-        [
-            jnp.concatenate([block(1, 3), block(2, 1).T], axis=1),
-            jnp.concatenate([block(2, 1), block(2, 3)], axis=1),
-        ],
-        axis=0,
+    stored, corner, side = block(1, 1), block(1, 3), block(1, 2)
+    special = cyclic(n)
+    last_diagonal = jnp.sum(jnp.where(special, stored, 0.0), axis=1, keepdims=True)
+    c_high, c_low = two_sum(block(1, 0), jnp.where(special, stored.T, stored))
+    rows, lanes = iota((n, n), 0), iota((n, n), 1)
+    turned_corner = corner.T
+    first_block = jnp.where(rows >= lanes, corner, turned_corner)
+    last_block = jnp.where(rows > lanes, turned_corner, jnp.where(rows < lanes, corner, last_diagonal))
+    excess = jnp.concatenate(
+        [jnp.concatenate([first_block, side.T], axis=1), jnp.concatenate([side, last_block], axis=1)], axis=0
     )
     eye_m = jnp.where(eye_mask(m), 1.0, 0.0)
-    t_high, t_error = two_sum(2.0 * eye_m, -g_high)
-    t_high, t_low = two_sum(t_high, t_error - g_low)
+    t_high, t_low = two_sum(eye_m, -excess)
 
     t_scale, t_inverse = power_of_two(jnp.max(jnp.max(jnp.abs(t_high), axis=1, keepdims=True), axis=0, keepdims=True))
     p_scale, p_inverse = power_of_two(jnp.max(jnp.abs(p_high), axis=0, keepdims=True))
@@ -345,26 +367,52 @@
     return weights, projector, novelty
 
 
-def finish_kernel(total_rows, packed_ref, values_ref, pair_ref, columns_ref, filtered_ref, projector_ref, novelty_ref, left):
+def finish_kernel(
+    total_rows,
+    packed_ref,
+    values_ref,
+    pair_hbm,
+    columns_hbm,
+    filtered_hbm,
+    projector_ref,
+    novelty_ref,
+    pair,
+    columns,
+    filtered,
+    arrived,
+    left_sem,
+):
     modes = values_ref.shape[1]
-
-    @pl.when(pl.program_id(0) == 0)
-    def _():
-        weights, projector, novelty = dense(packed_ref[...], values_ref[...], total_rows)
-        projector_ref[...] = projector
-        novelty_ref[...] = novelty
-        rounded = weights.astype(BF16)
-        rest = (weights - rounded.astype(F32)).astype(BF16)
-        left[...] = jnp.concatenate(
-            [rounded[:, 0:modes], rounded[:, 0:modes], rest[:, 0:modes], rounded[:, modes:], rest[:, modes:]], axis=1
+    lanes = pair.shape[1]
+    loads = [
+        pltpu.make_async_copy(pair_hbm, pair, arrived.at[0]),
+        pltpu.make_async_copy(columns_hbm, columns, arrived.at[1]),
+    ]
+    for load in loads:
+        load.start()
+    weights, projector, novelty = dense(sum_pairs(packed_ref), values_ref[...], total_rows)
+    rounded = weights.astype(BF16)
+    rest = (weights - rounded.astype(F32)).astype(BF16)
+    left = jnp.concatenate(
+        [rounded[:, 0:modes], rounded[:, 0:modes], rest[:, 0:modes], rounded[:, modes:], rest[:, modes:]], axis=1
+    )
+    for load in loads:
+        load.wait()
+    stores = []
+    for start in range(0, lanes, PIECE):
+        where = slice(start, start + PIECE)
+        first, second, third = pair[0:modes, where], pair[modes:, where], columns[:, where]
+        right = jnp.concatenate([first, second, first, third, third], axis=0)
+        filtered[:, where] = jnp.dot(left, right, preferred_element_type=F32)
+        store = pltpu.make_async_copy(
+            filtered.at[:, pl.ds(start, PIECE)], filtered_hbm.at[:, pl.ds(start, PIECE)], left_sem.at[len(stores)]
         )
-
-    lanes = filtered_ref.shape[1]
-    for start in range(0, lanes, 256):
-        where = slice(start, start + 256)
-        first, second, third = pair_ref[0:modes, where], pair_ref[modes:, where], columns_ref[:, where]
-        right = jnp.concatenate([first, second, first, third, third], axis=0)
-        filtered_ref[:, where] = jnp.dot(left[...], right, preferred_element_type=F32)
+        store.start()
+        stores.append(store)
+    projector_ref[...] = projector
+    novelty_ref[...] = novelty
+    for store in stores:
+        store.wait()
 
 
 def vmem(count):
@@ -375,15 +423,15 @@
     return jax.ShapeDtypeStruct(dims, dtype)
 
 
-def prepare(basis):
+def prepare(basis, share):
     modes, lanes = basis.shape
     return pl.pallas_call(
-        modes_kernel,
+        functools.partial(modes_kernel, share),
         out_shape=(
             shape((MODE_SLICES * modes, lanes), BF16),
             shape((modes, 1)),
             shape((2 * modes, lanes), BF16),
-            shape((2, modes, modes)),
+            shape((modes, modes)),
         ),
         in_specs=vmem(1),
         out_specs=tuple(vmem(4)),
@@ -392,36 +440,27 @@
     )(basis)
 
 
-def gather(ids, everything, parts, scale, gram):
+def gather(ids, everything, parts, scale, gram, copies):
     count, lanes = ids.shape[0], everything.shape[1]
     return pl.pallas_call(
         columns_kernel,
-        out_shape=(shape((count, lanes), BF16), shape((3 * count, 128))),
-        in_specs=vmem(5),
+        out_shape=(shape((count, lanes), BF16), shape((copies, 2 * count, 128))),
+        in_specs=vmem(2) + [pl.BlockSpec(memory_space=pl.ANY)] + vmem(2),
         out_specs=tuple(vmem(2)),
-        scratch_shapes=[pltpu.VMEM((COLUMN_SLICES * count, lanes), BF16)],
+        scratch_shapes=[
+            pltpu.VMEM((COLUMN_SLICES * count, lanes), BF16),
+            pltpu.VMEM(parts.shape, BF16),
+            pltpu.SemaphoreType.DMA((lanes // CHUNK,)),
+        ],
         interpret=INTERPRET,
         name="columns",
     )(ids, everything, parts, scale, gram)
 
 
-def take_half(place, both, copies):
-    rows = both.shape[1] // 2
-    return pl.pallas_call(
-        half_kernel,
-        out_shape=shape((copies, rows, 128)),
-        in_specs=[pl.BlockSpec(memory_space=pltpu.SMEM)] + vmem(1),
-        out_specs=vmem(1)[0],
-        interpret=INTERPRET,
-        name="half",
-    )(place, both)
-
-
 def add_up(parts, copies):
-    rows = parts.shape[1]
     return pl.pallas_call(
         sum_kernel,
-        out_shape=shape((rows, 128) if copies is None else (copies, rows, 128)),
+        out_shape=shape((copies,) + parts.shape[1:]),
         in_specs=vmem(1),
         out_specs=vmem(1)[0],
         interpret=INTERPRET,
@@ -430,49 +469,45 @@
 
 
 def finish(total_rows, packed, values, pair, columns):
-    import functools
-
     modes, count, lanes = values.shape[1], columns.shape[0], columns.shape[1]
     width = modes + count
-    steps = 4
+    anywhere = pl.BlockSpec(memory_space=pl.ANY)
     return pl.pallas_call(
         functools.partial(finish_kernel, total_rows),
-        grid=(steps,),
         out_shape=(shape((width, lanes)), shape((width, width)), shape((1, count))),
-        in_specs=[
-            pl.BlockSpec((3 * count, 128), lambda i: (0, 0)),
-            pl.BlockSpec((1, modes), lambda i: (0, 0)),
-            pl.BlockSpec((2 * modes, lanes // steps), lambda i: (0, i)),
-            pl.BlockSpec((count, lanes // steps), lambda i: (0, i)),
+        in_specs=vmem(2) + [anywhere, anywhere],
+        out_specs=(anywhere,) + tuple(vmem(2)),
+        scratch_shapes=[
+            pltpu.VMEM(pair.shape, BF16),
+            pltpu.VMEM(columns.shape, BF16),
+            pltpu.VMEM((width, lanes), F32),
+            pltpu.SemaphoreType.DMA((2,)),
+            pltpu.SemaphoreType.DMA((lanes // PIECE,)),
         ],
-        out_specs=(
-            pl.BlockSpec((width, lanes // steps), lambda i: (0, i)),
-            pl.BlockSpec((width, width), lambda i: (0, 0)),
-            pl.BlockSpec((1, count), lambda i: (0, 0)),
-        ),
-        scratch_shapes=[pltpu.VMEM((width, 256), BF16)],
         interpret=INTERPRET,
         name="finish",
     )(packed, values, pair, columns)
 
 
 def exchange(copies, axes):
-    return lax.all_to_all(copies, axes, 0, 0, tiled=True)
+    return near(lax.all_to_all(copies, axes, 0, 0, tiled=True))
+
+
+def near(array):
+    return pltpu.with_memory_space_constraint(array, pltpu.VMEM)
 
 
 def per_device(basis, values, archive, window_ids):
-    total_rows = basis.shape[1]
+    devices = 1
     for name in ALL:
-        total_rows *= lax.axis_size(name)
-    everything = lax.all_to_all(archive, ("x", "c"), split_axis=1, concat_axis=0, tiled=True)
-    parts, scale, pair, gram = prepare(basis)
-    columns, packed = gather(window_ids[:, None], everything, parts, scale, gram)
-    both = lax.all_gather(packed, "c")
-    plane = lax.axis_size("y") * lax.axis_size("x")
-    place = lax.axis_index("c").astype(jnp.int32)[None]
-    first = exchange(take_half(place, both, plane), ("y", "x"))
-    second = exchange(add_up(first, lax.axis_size("z")), ("z",))
-    packed = lax.all_gather(add_up(second, None), "c", tiled=True)
+        devices *= lax.axis_size(name)
+    total_rows = basis.shape[1] * devices
+    everything = near(lax.all_to_all(archive, ("x", "c"), split_axis=1, concat_axis=0, tiled=True))
+    parts, scale, pair, gram = prepare(basis, 1.0 / devices)
+    columns, packed = gather(window_ids[:, None], everything, parts, scale, gram, lax.axis_size("y"))
+    packed = add_up(exchange(packed, ("y",)), lax.axis_size("z"))
+    packed = add_up(exchange(packed, ("z",)), lax.axis_size("x") * lax.axis_size("c"))
+    packed = exchange(packed, ("x", "c"))
     filtered, projector, novelty = finish(total_rows, packed, values[None, :], pair, columns)
     return (filtered, projector, novelty.reshape(-1))
 

time: 96.4 us -> 81.9 us (0.85)
  blocking collectives: 54.4 us -> 45.8 us
  Pallas kernels: 24.1 us -> 19.2 us
    all_gather x2 -> x0, blocking collectives: 10.5 us -> none  [the longest x1 6.4 us: per_device(): packed = lax.all_gather(add_up(second, None), 'c', tiled=True)]
    pallas_call x5 -> x4, Pallas kernels: 19.2 us -> 14.2 us  [the longest x1 8.6 us: finish(): pl.pallas_call(functools.partial(finish_kernel, total_rows), out_shape=(s...]
    all_to_all x2 -> x3, blocking collectives: 43.9 us -> 45.8 us  [exchange(): return near(lax.all_to_all(copies, axes, 0, 0, tiled=True))]
  transfers between devices with their start and end apart: 1 -> 1, of which waited for: 1 -> 1; matrix products, arithmetic and copies ran while one was open for 1% -> 2% of each run, Pallas kernels for 4% -> 5%
where the time goes in v3:
time: 81.9 us; the launch traced here: 81.3 us
  blocking collectives  45.8 us (56%)
  Pallas kernels  19.2 us (23%)
  starting transfers between devices  10.2 us (12%)
  waiting for transfers between devices  4.09 us (5%)
  local copies, waits for them, and re-layouts  1.33 us (2%)
    all_to_all x3, blocking collectives, exchange(): return near(lax.all_to_all(copies, axes, 0, 0, tiled=True))  45.8 us
    all_to_all x1, starting transfers between devices, per_device(): lax.all_to_all(archive, ('x', 'c'), split_axis=1, concat_axis=0, tiled=True)  10.2 us
    pallas_call x1, Pallas kernels, finish(): pl.pallas_call(functools.partial(finish_kernel, total_rows), out_shape=(s...  8.6 us
    pallas_call x1, Pallas kernels, gather(): pl.pallas_call(columns_kernel, out_shape=(shape((count, lanes), BF16), sh...  4.97 us
    all_to_all x1, waiting for transfers between devices, per_device(): lax.all_to_all(archive, ('x', 'c'), split_axis=1, concat_axis=0, tiled=True)  4.09 us
    pallas_call x1, Pallas kernels, prepare(): pl.pallas_call(functools.partial(modes_kernel, share), out_shape=(shape((...  3.96 us
    pallas_call x2, Pallas kernels, add_up(): pl.pallas_call(sum_kernel, out_shape=shape((copies,) + parts.shape[1:]),...  1.66 us
  transfers between devices with their start and end apart: 1, of which 1 were waited for; matrix products, arithmetic and copies ran while one was open for 2% of the time, Pallas kernels for 5%

profile of v3, /device:TPU:1, one launch (start us, length us, event | category | flops | bytes accessed | tf_op | source)
XLA Modules:
  0.0 81.3 jit_solution(10770798051096862880)
XLA Ops:
  0.6 10.2 %all-to-all-start = ((bf16[8,8,4096]{2,0,1:T(8,128)(2,1)}), bf16[8,8,4096]{2,0,1:T(8,128)(2,1)S(1)}, u32[]{:S(2)}, u32[]{:S(2)}) async-start(bf16[8,8,4096]{2,0,1:T(8,128)(2,1)} %bitcast.8), calls=%async_computation | async-start | bytes 1048576 | tf_op jit(solution)/shard_map/all_to_all | solution.py:505
  10.9 1.3 %copy.7.ids_ref = s32[32,1]{1,0:T(8,128)} copy(s32[32,1]{0,1:T(1,128)} %bitcast.10) | data formatting | bytes 256 | tf_op jit(solution)/shard_map/broadcast_in_dim | solution.py:507
  12.2 4.0 %modes.1 = (bf16[256,4096]{1,0:T(8,128)(2,1)}, f32[64,1]{1,0:T(8,128)}, bf16[128,4096]{1,0:T(8,128)(2,1)}, f32[64,64]{1,0:T(8,128)}) custom-call(f32[64,4096]{1,0:T(8,128)} %basis_ref.1), custom_call_target="tpu_custom_call" | custom-call | tf_op jit(solution)/shard_map/modes/pallas_call | solution.py:428
  16.2 4.1 %all-to-all-done = bf16[8,8,4096]{2,0,1:T(8,128)(2,1)S(1)} async-done(((bf16[8,8,4096]{2,0,1:T(8,128)(2,1)}), bf16[8,8,4096]{2,0,1:T(8,128)(2,1)S(1)}, u32[]{:S(2)}, u32[]{:S(2)}) %all-to-all-start) | async-done | bytes 524320 | tf_op jit(solution)/shard_map/all_to_all | solution.py:505
  20.3 5.0 %columns.1 = (bf16[32,4096]{1,0:T(8,128)(2,1)}, f32[8,64,128]{2,1,0:T(8,128)}) custom-call(s32[32,1]{1,0:T(8,128)} %copy.7.ids_ref, bf16[64,4096]{1,0:T(8,128)(2,1)S(1)} %bitcast.7, bf16[256,4096]{1,0:T(8,128)(2,1)} %get-tuple-element.12.parts_hbm, f32[64,1]{1,0:T(8,128)} %get-tuple-element.13.scale_ref, f32[64,64]{1,0:T(8,128)} %get-tuple-element.14.gram_ref), custom_call_target="tpu_custom_call" | custom-call | tf_op jit(solution)/shard_map/columns/pallas_call | solution.py:445
  25.2 13.8 %all_to_all.34.parts_ref = f32[8,64,128]{2,1,0:T(8,128)S(1)} all-to-all(f32[8,64,128]{2,1,0:T(8,128)} %get-tuple-element.15), channel_id=1, replica_groups=mesh['y'=8,'z'=8,'x'=4,'c'=2] {'y'}, dimensions={0} | all-to-all | bytes 524288 | tf_op jit(solution)/shard_map/all_to_all | solution.py:493
  39.1 0.8 %add.2 = f32[8,64,128]{2,1,0:T(8,128)} custom-call(f32[8,64,128]{2,1,0:T(8,128)S(1)} %all_to_all.34.parts_ref), custom_call_target="tpu_custom_call" | custom-call | tf_op jit(solution)/shard_map/add/pallas_call | solution.py:461
  39.9 18.2 %all_to_all.35.parts_ref = f32[8,64,128]{2,1,0:T(8,128)S(1)} all-to-all(f32[8,64,128]{2,1,0:T(8,128)} %add.2), channel_id=1, replica_groups=mesh['y'=8,'z'=8,'x'=4,'c'=2] {'z'}, dimensions={0} | all-to-all | bytes 524288 | tf_op jit(solution)/shard_map/all_to_all | solution.py:493
  58.1 0.8 %add.3 = f32[8,64,128]{2,1,0:T(8,128)} custom-call(f32[8,64,128]{2,1,0:T(8,128)S(1)} %all_to_all.35.parts_ref), custom_call_target="tpu_custom_call" | custom-call | tf_op jit(solution)/shard_map/add/pallas_call | solution.py:461
  58.9 13.8 %all_to_all.36.packed_ref = f32[8,64,128]{2,1,0:T(8,128)S(1)} all-to-all(f32[8,64,128]{2,1,0:T(8,128)} %add.3), channel_id=1, replica_groups=mesh['y'=8,'z'=8,'x'=4,'c'=2] {'x','c'}, dimensions={0} | all-to-all | bytes 524288 | tf_op jit(solution)/shard_map/all_to_all | solution.py:493
  72.7 8.6 %finish.1 = (f32[96,4096]{1,0:T(8,128)}, f32[96,96]{1,0:T(8,128)}, f32[1,32]{1,0:T(1,128)}) custom-call(f32[8,64,128]{2,1,0:T(8,128)S(1)} %all_to_all.36.packed_ref, f32[1,64]{1,0:T(1,128)} %bitcast.9, bf16[128,4096]{1,0:T(8,128)(2,1)} %get-tuple-element.16.pair_hbm, bf16[32,4096]{1,0:T(8,128)(2,1)} %get-tuple-element.17.columns_hbm), custom_call_target="tpu_custom_call" | custom-call | tf_op jit(solution)/shard_map/finish/pallas_call | solution.py:475
Async XLA Ops:
  0.6 19.6 %all-to-all-start = ((bf16[8,8,4096]{2,0,1:T(8,128)(2,1)}), bf16[8,8,4096]{2,0,1:T(8,128)(2,1)S(1)}, u32[]{:S(2)}, u32[]{:S(2)}) async-start(bf16[8,8,4096]{2,0,1:T(8,128)(2,1)} %bitcast.8), calls=%async_computation | async-start | bytes 1048576 | tf_op jit(solution)/shard_map/all_to_all | solution.py:505

commit v4 on v3

--- a/solution.py
+++ b/solution.py
@@ -166,20 +166,12 @@
 
 
 def columns_kernel(
-    ids_ref, archive_ref, parts_hbm, scale_ref, gram_ref, columns_ref, packed_ref, slices, parts, arrived
+    ids_ref, archive_ref, parts, scale_ref, gram_ref, columns_ref, packed_ref, slices
 ):
     count = ids_ref.shape[0]
     total, lanes = archive_ref.shape
     modes = scale_ref.shape[0]
     starts = range(0, lanes, CHUNK)
-    copies = [
-        pltpu.make_async_copy(
-            parts_hbm.at[:, pl.ds(start, CHUNK)], parts.at[:, pl.ds(start, CHUNK)], arrived.at[index]
-        )
-        for index, start in enumerate(starts)
-    ]
-    for copy in copies:
-        copy.start()
     picker = jnp.where(ids_ref[...] == iota((count, total), 1), 1.0, 0.0).astype(BF16)
     bound = jnp.zeros((count, 1), F32)
     for start in range(0, lanes, PIECE):
@@ -194,8 +186,7 @@
 
     whole, lead_p, lead_c = None, [], []
     height = MODE_SLICES * modes
-    for start, copy in zip(starts, copies):
-        copy.wait()
+    for start in starts:
         right = slices[:, start : start + CHUNK]
         product = dot_nt(jnp.concatenate([parts[:, start : start + CHUNK], right], axis=0), right)
         lead_p.append(product[0:modes, 0:count])
@@ -249,6 +240,31 @@
     return jnp.dot(a, b, precision=HIGH, preferred_element_type=F32)
 
 
+def widen(a):
+    return jnp.concatenate([a, jnp.zeros((a.shape[0], 128 - a.shape[1]), F32)], axis=1)
+
+
+def pieces_of(a):
+    high = a.astype(BF16)
+    rest = a - high.astype(F32)
+    middle = rest.astype(BF16)
+    return high, middle, (rest - middle.astype(F32)).astype(BF16)
+
+
+def wide_dot(left, right):
+    a_high, a_middle, a_low = left
+    b_high, b_middle, b_low = right
+    none = jnp.zeros((128 - b_high.shape[0], 128), BF16)
+
+    def long_dot(across, down):
+        down = [block for piece in down for block in (piece, none)]
+        return jnp.dot(jnp.concatenate(across, axis=1), jnp.concatenate(down, axis=0), preferred_element_type=F32)
+
+    return long_dot((a_low, a_high, a_middle), (b_high, b_low, b_middle)) + long_dot(
+        (a_middle, a_high, a_high), (b_high, b_middle, b_high)
+    )
+
+
 def slice_product(left, right, level_count):
     size = left[0].shape[0]
     stacked = jnp.concatenate(left, axis=0).astype(BF16)
@@ -339,17 +355,18 @@
     inner = jnp.concatenate([kernel_top, kernel_low], axis=0)
     eye_w = jnp.where(eye_mask(width), 1.0, 0.0)
     total = jnp.sum(jnp.sum(inner * eye_w, axis=1, keepdims=True), axis=0, keepdims=True)
-    shifted = (inner - (total / width) * eye_w) / total
-    slope = eye_w
+    shifted = widen((inner - (total / width) * eye_w) / total)
+    slope = eye = widen(eye_w)
     origin = -1.0 / width
     for _ in range(NEWTON):
-        squared = high_dot(shifted, shifted)
-        divided = (origin * origin) * eye_w + origin * shifted + squared
-        slope = 1.5 * slope - 0.5 * high_dot(slope, divided)
-        shifted = 1.5 * shifted - 0.5 * high_dot(shifted, squared)
+        pieces = pieces_of(shifted)
+        squared = wide_dot(pieces, pieces)
+        divided = (origin * origin) * eye + origin * shifted + squared
+        slope = 1.5 * slope - 0.5 * wide_dot(pieces_of(slope), pieces_of(divided))
+        shifted = 1.5 * shifted - 0.5 * wide_dot(pieces, pieces_of(squared))
         origin = 1.5 * origin - 0.5 * origin * origin * origin
-    blend = 0.5 * (eye_w + shifted)
-    slope = slope * (0.5 / total)
+    blend = 0.5 * (eye_w + shifted[:, 0:width])
+    slope = slope[:, 0:width] * (0.5 / total)
 
     upper = triangle(one_high, one_low) * scale
     core = jnp.concatenate(
@@ -371,33 +388,22 @@
     total_rows,
     packed_ref,
     values_ref,
-    pair_hbm,
-    columns_hbm,
+    pair,
+    columns,
     filtered_hbm,
     projector_ref,
     novelty_ref,
-    pair,
-    columns,
     filtered,
-    arrived,
     left_sem,
 ):
     modes = values_ref.shape[1]
     lanes = pair.shape[1]
-    loads = [
-        pltpu.make_async_copy(pair_hbm, pair, arrived.at[0]),
-        pltpu.make_async_copy(columns_hbm, columns, arrived.at[1]),
-    ]
-    for load in loads:
-        load.start()
     weights, projector, novelty = dense(sum_pairs(packed_ref), values_ref[...], total_rows)
     rounded = weights.astype(BF16)
     rest = (weights - rounded.astype(F32)).astype(BF16)
     left = jnp.concatenate(
         [rounded[:, 0:modes], rounded[:, 0:modes], rest[:, 0:modes], rounded[:, modes:], rest[:, modes:]], axis=1
     )
-    for load in loads:
-        load.wait()
     stores = []
     for start in range(0, lanes, PIECE):
         where = slice(start, start + PIECE)
@@ -423,19 +429,28 @@
     return jax.ShapeDtypeStruct(dims, dtype)
 
 
+def kept(dims, dtype=F32):
+    return shape(dims, dtype) if INTERPRET else pltpu.VMEM(dims, dtype)
+
+
+def params():
+    return pltpu.CompilerParams(vmem_limit_bytes=24 * 1024 * 1024)
+
+
 def prepare(basis, share):
     modes, lanes = basis.shape
     return pl.pallas_call(
         functools.partial(modes_kernel, share),
         out_shape=(
-            shape((MODE_SLICES * modes, lanes), BF16),
-            shape((modes, 1)),
-            shape((2 * modes, lanes), BF16),
-            shape((modes, modes)),
+            kept((MODE_SLICES * modes, lanes), BF16),
+            kept((modes, 1)),
+            kept((2 * modes, lanes), BF16),
+            kept((modes, modes)),
         ),
         in_specs=vmem(1),
         out_specs=tuple(vmem(4)),
         interpret=INTERPRET,
+        compiler_params=params(),
         name="modes",
     )(basis)
 
@@ -444,15 +459,14 @@
     count, lanes = ids.shape[0], everything.shape[1]
     return pl.pallas_call(
         columns_kernel,
-        out_shape=(shape((count, lanes), BF16), shape((copies, 2 * count, 128))),
-        in_specs=vmem(2) + [pl.BlockSpec(memory_space=pl.ANY)] + vmem(2),
+        out_shape=(kept((count, lanes), BF16), kept((copies, 2 * count, 128))),
+        in_specs=vmem(5),
         out_specs=tuple(vmem(2)),
         scratch_shapes=[
             pltpu.VMEM((COLUMN_SLICES * count, lanes), BF16),
-            pltpu.VMEM(parts.shape, BF16),
-            pltpu.SemaphoreType.DMA((lanes // CHUNK,)),
         ],
         interpret=INTERPRET,
+        compiler_params=params(),
         name="columns",
     )(ids, everything, parts, scale, gram)
 
@@ -460,10 +474,11 @@
 def add_up(parts, copies):
     return pl.pallas_call(
         sum_kernel,
-        out_shape=shape((copies,) + parts.shape[1:]),
+        out_shape=kept((copies,) + parts.shape[1:]),
         in_specs=vmem(1),
         out_specs=vmem(1)[0],
         interpret=INTERPRET,
+        compiler_params=params(),
         name="add",
     )(parts)
 
@@ -475,16 +490,14 @@
     return pl.pallas_call(
         functools.partial(finish_kernel, total_rows),
         out_shape=(shape((width, lanes)), shape((width, width)), shape((1, count))),
-        in_specs=vmem(2) + [anywhere, anywhere],
+        in_specs=vmem(4),
         out_specs=(anywhere,) + tuple(vmem(2)),
         scratch_shapes=[
-            pltpu.VMEM(pair.shape, BF16),
-            pltpu.VMEM(columns.shape, BF16),
             pltpu.VMEM((width, lanes), F32),
-            pltpu.SemaphoreType.DMA((2,)),
             pltpu.SemaphoreType.DMA((lanes // PIECE,)),
         ],
         interpret=INTERPRET,
+        compiler_params=params(),
         name="finish",
     )(packed, values, pair, columns)
 
@@ -504,11 +517,11 @@
     total_rows = basis.shape[1] * devices
     everything = near(lax.all_to_all(archive, ("x", "c"), split_axis=1, concat_axis=0, tiled=True))
     parts, scale, pair, gram = prepare(basis, 1.0 / devices)
-    columns, packed = gather(window_ids[:, None], everything, parts, scale, gram, lax.axis_size("y"))
+    columns, packed = gather(near(window_ids[:, None]), everything, parts, scale, gram, lax.axis_size("y"))
     packed = add_up(exchange(packed, ("y",)), lax.axis_size("z"))
     packed = add_up(exchange(packed, ("z",)), lax.axis_size("x") * lax.axis_size("c"))
     packed = exchange(packed, ("x", "c"))
-    filtered, projector, novelty = finish(total_rows, packed, values[None, :], pair, columns)
+    filtered, projector, novelty = finish(total_rows, packed, near(values[None, :]), pair, columns)
     return (filtered, projector, novelty.reshape(-1))
 
 

time: 81.9 us -> 74.5 us (0.910)
  Pallas kernels: 19.2 us -> 11.4 us
  local copies, waits for them, and re-layouts: 1.33 us -> 2.93 us
  blocking collectives: 45.8 us -> 44.4 us
    pallas_call x4, Pallas kernels: 10.6 us -> 3.77 us  [the longest x1 1.91 us: prepare(): pl.pallas_call(functools.partial(modes_kernel, share), out_shape=(kept((M...]
    unnamed x0 -> x8, local copies, waits for them, and re-layouts: none -> 2.2 us
    all_to_all x3, blocking collectives: 45.8 us -> 44.4 us  [exchange(): return near(lax.all_to_all(copies, axes, 0, 0, tiled=True))]
    pallas_call x1, Pallas kernels: 8.6 us -> 7.62 us  [finish(): pl.pallas_call(functools.partial(finish_kernel, total_rows), out_shape=(s...]
  transfers between devices with their start and end apart: 1 -> 1, of which waited for: 1 -> 1; matrix products, arithmetic and copies ran while one was open for 2% -> 1% of each run, Pallas kernels for 5% -> 3%
where the time goes in v4:
time: 74.5 us; the launch traced here: 74.2 us
  blocking collectives  44.4 us (60%)
  Pallas kernels  11.4 us (15%)
  starting transfers between devices  10.2 us (14%)
  waiting for transfers between devices  4.53 us (6%)
  local copies, waits for them, and re-layouts  2.93 us (4%)
    all_to_all x3, blocking collectives, exchange(): return near(lax.all_to_all(copies, axes, 0, 0, tiled=True))  44.4 us
    all_to_all x1, starting transfers between devices, per_device(): lax.all_to_all(archive, ('x', 'c'), split_axis=1, concat_axis=0, tiled=True)  10.2 us
    pallas_call x1, Pallas kernels, finish(): pl.pallas_call(functools.partial(finish_kernel, total_rows), out_shape=(s...  7.62 us
    all_to_all x1, waiting for transfers between devices, per_device(): lax.all_to_all(archive, ('x', 'c'), split_axis=1, concat_axis=0, tiled=True)  4.53 us
    unnamed x8, local copies, waits for them, and re-layouts  2.2 us
    pallas_call x1, Pallas kernels, prepare(): pl.pallas_call(functools.partial(modes_kernel, share), out_shape=(kept((M...  1.91 us
    pallas_call x1, Pallas kernels, gather(): pl.pallas_call(columns_kernel, out_shape=(kept((count, lanes), BF16), kep...  1.6 us
  transfers between devices with their start and end apart: 1, of which 1 were waited for; matrix products, arithmetic and copies ran while one was open for 1% of the time, Pallas kernels for 3%

profile of v4, /device:TPU:1, one launch (start us, length us, event | category | flops | bytes accessed | tf_op | source)
XLA Modules:
  0.0 74.2 jit_solution(17829844288780740571)
XLA Ops:
  0.6 10.2 %all-to-all-start = ((bf16[8,8,4096]{2,0,1:T(8,128)(2,1)}), bf16[8,8,4096]{2,0,1:T(8,128)(2,1)S(1)}, u32[]{:S(2)}, u32[]{:S(2)}) async-start(bf16[8,8,4096]{2,0,1:T(8,128)(2,1)} %bitcast.9), calls=%async_computation | async-start | bytes 1048576 | tf_op jit(solution)/shard_map/all_to_all | solution.py:518
  10.9 0.7 copy.7.ids_ref
  11.6 0.0 copy-start
  11.6 1.2 %copy-done = f32[64,4096]{1,0:T(8,128)S(1)} copy-done((f32[64,4096]{1,0:T(8,128)S(1)}, f32[64,4096]{1,0:T(8,128)}, u32[]{:S(2)}) %copy-start) | copy-done | bytes 1048600
  12.8 1.9 %modes.1 = (bf16[256,4096]{1,0:T(8,128)(2,1)S(1)}, f32[64,1]{1,0:T(8,128)S(1)}, bf16[128,4096]{1,0:T(8,128)(2,1)S(1)}, f32[64,64]{1,0:T(8,128)S(1)}) custom-call(f32[64,4096]{1,0:T(8,128)S(1)} %copy-done), custom_call_target="tpu_custom_call" | custom-call | tf_op jit(solution)/shard_map/modes/pallas_call | solution.py:442
  14.8 0.0 copy-start.1
  14.8 1.0 %copy-done.1 = bf16[128,4096]{1,0:T(8,128)(2,1)} copy-done((bf16[128,4096]{1,0:T(8,128)(2,1)}, bf16[128,4096]{1,0:T(8,128)(2,1)S(1)}, u32[]{:S(2)}) %copy-start.1) | copy-done | bytes 1048600
  15.7 4.5 %all-to-all-done = bf16[8,8,4096]{2,0,1:T(8,128)(2,1)S(1)} async-done(((bf16[8,8,4096]{2,0,1:T(8,128)(2,1)}), bf16[8,8,4096]{2,0,1:T(8,128)(2,1)S(1)}, u32[]{:S(2)}, u32[]{:S(2)}) %all-to-all-start) | async-done | bytes 524320 | tf_op jit(solution)/shard_map/all_to_all | solution.py:518
  20.3 0.0 copy-start.2
  20.3 0.0 copy-start.3
  20.3 1.6 %columns.1 = (bf16[32,4096]{1,0:T(8,128)(2,1)S(1)}, f32[8,64,128]{2,1,0:T(8,128)S(1)}) custom-call(s32[32,1]{1,0:T(8,128)S(1)} %copy.7.ids_ref, bf16[64,4096]{1,0:T(8,128)(2,1)S(1)} %bitcast.7, bf16[256,4096]{1,0:T(8,128)(2,1)S(1)} %get-tuple-element.12.parts, f32[64,1]{1,0:T(8,128)S(1)} %get-tuple-element.13.scale_ref, f32[64,64]{1,0:T(8,128)S(1)} %get-tuple-element.14.gram_ref), custom_call_target="tpu_custom_call" | custom-call | tf_op jit(solution)/shard_map/columns/pallas_call | solution.py:460
  21.9 12.9 %all_to_all.34.parts_ref = f32[8,64,128]{2,1,0:T(8,128)S(1)} all-to-all(f32[8,64,128]{2,1,0:T(8,128)S(1)} %get-tuple-element.15), channel_id=1, replica_groups=mesh['y'=8,'z'=8,'x'=4,'c'=2] {'y'}, dimensions={0} | all-to-all | bytes 524288 | tf_op jit(solution)/shard_map/all_to_all | solution.py:506
  34.8 0.1 add.2
  34.9 18.6 %all_to_all.35.parts_ref = f32[8,64,128]{2,1,0:T(8,128)S(1)} all-to-all(f32[8,64,128]{2,1,0:T(8,128)S(1)} %add.2), channel_id=1, replica_groups=mesh['y'=8,'z'=8,'x'=4,'c'=2] {'z'}, dimensions={0} | all-to-all | bytes 524288 | tf_op jit(solution)/shard_map/all_to_all | solution.py:506
  53.6 0.1 add.3
  53.7 12.9 %all_to_all.36.packed_ref = f32[8,64,128]{2,1,0:T(8,128)S(1)} all-to-all(f32[8,64,128]{2,1,0:T(8,128)S(1)} %add.3), channel_id=1, replica_groups=mesh['y'=8,'z'=8,'x'=4,'c'=2] {'x','c'}, dimensions={0} | all-to-all | bytes 524288 | tf_op jit(solution)/shard_map/all_to_all | solution.py:506
  66.6 0.0 copy-done.2
  66.6 0.0 copy-done.3
  66.6 7.6 %finish.1 = (f32[96,4096]{1,0:T(8,128)}, f32[96,96]{1,0:T(8,128)}, f32[1,32]{1,0:T(1,128)}) custom-call(f32[8,64,128]{2,1,0:T(8,128)S(1)} %all_to_all.36.packed_ref, f32[1,64]{1,0:T(1,128)S(1)} %bitcast.8, bf16[128,4096]{1,0:T(8,128)(2,1)S(1)} %copy-done.2, bf16[32,4096]{1,0:T(8,128)(2,1)S(1)} %get-tuple-element.17.columns), custom_call_target="tpu_custom_call" | custom-call | tf_op jit(solution)/shard_map/finish/pallas_call | solution.py:490
Async XLA Ops:
  0.6 19.6 %all-to-all-start = ((bf16[8,8,4096]{2,0,1:T(8,128)(2,1)}), bf16[8,8,4096]{2,0,1:T(8,128)(2,1)S(1)}, u32[]{:S(2)}, u32[]{:S(2)}) async-start(bf16[8,8,4096]{2,0,1:T(8,128)(2,1)} %bitcast.9), calls=%async_computation | async-start | bytes 1048576 | tf_op jit(solution)/shard_map/all_to_all | solution.py:518
  11.6 1.2 %copy-start = (f32[64,4096]{1,0:T(8,128)S(1)}, f32[64,4096]{1,0:T(8,128)}, u32[]{:S(2)}) copy-start(f32[64,4096]{1,0:T(8,128)} %basis_ref.1) | copy-start | bytes 3145732
  14.8 1.0 %copy-start.1 = (bf16[128,4096]{1,0:T(8,128)(2,1)}, bf16[128,4096]{1,0:T(8,128)(2,1)S(1)}, u32[]{:S(2)}) copy-start(bf16[128,4096]{1,0:T(8,128)(2,1)S(1)} %get-tuple-element.16.pair) | copy-start | bytes 3145732
  20.3 46.3 %copy-start.2 = (bf16[128,4096]{1,0:T(8,128)(2,1)S(1)}, bf16[128,4096]{1,0:T(8,128)(2,1)}, u32[]{:S(2)}) copy-start(bf16[128,4096]{1,0:T(8,128)(2,1)} %copy-done.1) | copy-start | bytes 3145732
  20.3 46.3 %copy-start.3 = (f32[64]{0:T(128)S(1)}, f32[64]{0:T(128)}, u32[]{:S(2)}) copy-start(f32[64]{0:T(128)} %param.5) | copy-start | bytes 772

commit v5 on v4

--- a/solution.py
+++ b/solution.py
@@ -215,23 +215,32 @@
         packed_ref[index, n:, :] = low
 
 
-def sum_pairs(parts_ref):
-    high = parts_ref[0]
+def sum_pairs(load, count, place, n):
+    high = load(0)
     error = jnp.zeros_like(high)
-    for index in range(1, parts_ref.shape[0]):
-        high, part = two_sum(high, parts_ref[index])
+    for index in range(1, count):
+        high, part = two_sum(high, load(index))
         error = error + part
-    n = high.shape[0] // 2
     rows, lanes = iota(high.shape, 0), iota(high.shape, 1)
-    top_takes = (rows < n) & ((lanes // n) % 2 == 1)
-    row, lane = rows - n, lanes - n
-    special = (lane == row + 1) | ((row == n - 1) & (lane == 0))
-    takes = top_takes | ((row >= 0) & (lane >= 0) & (lane < n) & jnp.logical_not(special))
-    return jnp.where(takes, high + pltpu.roll(error, n, 1), high)
-
-
-def sum_kernel(parts_ref, out_ref):
-    total = sum_pairs(parts_ref)
+    top_takes = (lanes // n) % 2 == 1
+    lane = lanes - n
+    special = (lane == rows + 1) | ((rows == n - 1) & (lane == 0))
+    low_takes = (lane >= 0) & (lane < n) & jnp.logical_not(special)
+    takes = jnp.where(place == 0, jnp.where(top_takes, 1.0, 0.0), jnp.where(low_takes, 1.0, 0.0))
+    return high + takes * pltpu.roll(error, n, 1)
+
+
+def half_kernel(place_ref, both_ref, out_ref):
+    copies, rows, _ = out_ref.shape
+    start = pl.multiple_of(place_ref[0] * rows, 8)
+    total = sum_pairs(lambda index: both_ref[index, pl.ds(start, rows), :], both_ref.shape[0], place_ref[0], rows)
+    for index in range(copies):
+        out_ref[index] = total
+
+
+def sum_kernel(place_ref, parts_ref, out_ref):
+    rows = parts_ref.shape[1]
+    total = sum_pairs(lambda index: parts_ref[index], parts_ref.shape[0], place_ref[0], rows)
     for index in range(out_ref.shape[0]):
         out_ref[index] = total
 
@@ -246,23 +255,15 @@
 
 def pieces_of(a):
     high = a.astype(BF16)
-    rest = a - high.astype(F32)
-    middle = rest.astype(BF16)
-    return high, middle, (rest - middle.astype(F32)).astype(BF16)
+    return high, (a - high.astype(F32)).astype(BF16)
 
 
 def wide_dot(left, right):
-    a_high, a_middle, a_low = left
-    b_high, b_middle, b_low = right
+    a_high, a_low = left
+    b_high, b_low = right
     none = jnp.zeros((128 - b_high.shape[0], 128), BF16)
-
-    def long_dot(across, down):
-        down = [block for piece in down for block in (piece, none)]
-        return jnp.dot(jnp.concatenate(across, axis=1), jnp.concatenate(down, axis=0), preferred_element_type=F32)
-
-    return long_dot((a_low, a_high, a_middle), (b_high, b_low, b_middle)) + long_dot(
-        (a_middle, a_high, a_high), (b_high, b_middle, b_high)
-    )
+    down = jnp.concatenate([b_high, none, b_low, none, b_high, none], axis=0)
+    return jnp.dot(jnp.concatenate([a_low, a_high, a_high], axis=1), down, preferred_element_type=F32)
 
 
 def slice_product(left, right, level_count):
@@ -347,10 +348,10 @@
 
     values_column = to_column(values)
     projection = p_high * scale
-    gram = one_high * square_scale
     turned = projection.T
     mixed = projection * values_column
     kernel_top = jnp.concatenate([eye_m * (values_column * values_column), mixed], axis=1)
+    gram = one_high * square_scale
     kernel_low = jnp.concatenate([mixed.T, high_dot(turned, projection) + gram], axis=1)
     inner = jnp.concatenate([kernel_top, kernel_low], axis=0)
     eye_w = jnp.where(eye_mask(width), 1.0, 0.0)
@@ -398,7 +399,7 @@
 ):
     modes = values_ref.shape[1]
     lanes = pair.shape[1]
-    weights, projector, novelty = dense(sum_pairs(packed_ref), values_ref[...], total_rows)
+    weights, projector, novelty = dense(packed_ref[0], values_ref[...], total_rows)
     rounded = weights.astype(BF16)
     rest = (weights - rounded.astype(F32)).astype(BF16)
     left = jnp.concatenate(
@@ -471,16 +472,28 @@
     )(ids, everything, parts, scale, gram)
 
 
-def add_up(parts, copies):
+def add_up(place, parts, copies):
     return pl.pallas_call(
         sum_kernel,
         out_shape=kept((copies,) + parts.shape[1:]),
-        in_specs=vmem(1),
+        in_specs=[pl.BlockSpec(memory_space=pltpu.SMEM)] + vmem(1),
         out_specs=vmem(1)[0],
         interpret=INTERPRET,
         compiler_params=params(),
         name="add",
-    )(parts)
+    )(place, parts)
+
+
+def take_half(place, both, copies):
+    return pl.pallas_call(
+        half_kernel,
+        out_shape=kept((copies, both.shape[1] // 2, 128)),
+        in_specs=[pl.BlockSpec(memory_space=pltpu.SMEM)] + vmem(1),
+        out_specs=vmem(1)[0],
+        interpret=INTERPRET,
+        compiler_params=params(),
+        name="half",
+    )(place, both)
 
 
 def finish(total_rows, packed, values, pair, columns):
@@ -517,10 +530,14 @@
     total_rows = basis.shape[1] * devices
     everything = near(lax.all_to_all(archive, ("x", "c"), split_axis=1, concat_axis=0, tiled=True))
     parts, scale, pair, gram = prepare(basis, 1.0 / devices)
-    columns, packed = gather(near(window_ids[:, None]), everything, parts, scale, gram, lax.axis_size("y"))
-    packed = add_up(exchange(packed, ("y",)), lax.axis_size("z"))
-    packed = add_up(exchange(packed, ("z",)), lax.axis_size("x") * lax.axis_size("c"))
-    packed = exchange(packed, ("x", "c"))
+    columns, packed = gather(near(window_ids[:, None]), everything, parts, scale, gram, 1)
+    place = lax.axis_index("c").astype(jnp.int32)[None]
+    both = near(lax.all_gather(packed, "c", axis=0, tiled=True))
+    packed = take_half(place, both, lax.axis_size("y"))
+    packed = add_up(place, exchange(packed, ("y",)), lax.axis_size("z"))
+    packed = add_up(place, exchange(packed, ("z",)), lax.axis_size("x"))
+    packed = add_up(place, exchange(packed, ("x",)), 1)
+    packed = near(lax.all_gather(packed, "c", axis=1, tiled=True))
     filtered, projector, novelty = finish(total_rows, packed, near(values[None, :]), pair, columns)
     return (filtered, projector, novelty.reshape(-1))
 

time: 74.5 us -> 72.7 us (0.976)
  blocking collectives: 44.4 us -> 43.3 us
    all_to_all x3, blocking collectives: 44.4 us -> 34.8 us  [exchange(): return near(lax.all_to_all(copies, axes, 0, 0, tiled=True))]
    all_gather x0 -> x2, blocking collectives: none -> 8.52 us  [the longest x1 6.03 us: per_device(): packed = near(lax.all_gather(packed, 'c', axis=1, tiled=True))]
    pallas_call x1, Pallas kernels: 7.62 us -> 6.81 us  [finish(): pl.pallas_call(functools.partial(finish_kernel, total_rows), out_shape=(s...]
    unnamed x8 -> x10, local copies, waits for them, and re-layouts: 2.2 us -> 2.2 us
  transfers between devices with their start and end apart: 1 -> 1, of which waited for: 1 -> 1; matrix products, arithmetic and copies ran while one was open for 1% -> 0% of each run, Pallas kernels for 3% -> 3%
where the time goes in v5:
time: 72.7 us; the launch traced here: 72.4 us
  blocking collectives  43.3 us (60%)
  Pallas kernels  10.7 us (15%)
  starting transfers between devices  10.2 us (14%)
  waiting for transfers between devices  5.17 us (7%)
  local copies, waits for them, and re-layouts  2.29 us (3%)
    all_to_all x3, blocking collectives, exchange(): return near(lax.all_to_all(copies, axes, 0, 0, tiled=True))  34.8 us
    all_to_all x1, starting transfers between devices, per_device(): lax.all_to_all(archive, ('x', 'c'), split_axis=1, concat_axis=0, tiled=True)  10.2 us
    pallas_call x1, Pallas kernels, finish(): pl.pallas_call(functools.partial(finish_kernel, total_rows), out_shape=(s...  6.81 us
    all_gather x1, blocking collectives, per_device(): packed = near(lax.all_gather(packed, 'c', axis=1, tiled=True))  6.03 us
    all_to_all x1, waiting for transfers between devices, per_device(): lax.all_to_all(archive, ('x', 'c'), split_axis=1, concat_axis=0, tiled=True)  5.17 us
    all_gather x1, blocking collectives, per_device(): both = near(lax.all_gather(packed, 'c', axis=0, tiled=True))  2.49 us
    unnamed x10, local copies, waits for them, and re-layouts  2.2 us
    pallas_call x1, Pallas kernels, prepare(): pl.pallas_call(functools.partial(modes_kernel, share), out_shape=(kept((M...  1.91 us
  transfers between devices with their start and end apart: 1, of which 1 were waited for; matrix products, arithmetic and copies ran while one was open for 0% of the time, Pallas kernels for 3%

profile of v5, /device:TPU:1, one launch (start us, length us, event | category | flops | bytes accessed | tf_op | source)
XLA Modules:
  0.0 72.4 jit_solution(6459229584574241428)
XLA Ops:
  0.6 0.0 copy-start.4
  0.6 10.2 %all-to-all-start = ((bf16[8,8,4096]{2,0,1:T(8,128)(2,1)}), bf16[8,8,4096]{2,0,1:T(8,128)(2,1)S(1)}, u32[]{:S(2)}, u32[]{:S(2)}) async-start(bf16[8,8,4096]{2,0,1:T(8,128)(2,1)} %bitcast.10), calls=%async_computation | async-start | bytes 1048576 | tf_op jit(solution)/shard_map/all_to_all | solution.py:531
  10.9 0.0 copy-start.2
  10.9 1.2 %copy-done.2 = f32[64,4096]{1,0:T(8,128)S(1)} copy-done((f32[64,4096]{1,0:T(8,128)S(1)}, f32[64,4096]{1,0:T(8,128)}, u32[]{:S(2)}) %copy-start.2) | copy-done | bytes 1048600
  12.1 1.9 %modes.1 = (bf16[256,4096]{1,0:T(8,128)(2,1)S(1)}, f32[64,1]{1,0:T(8,128)S(1)}, bf16[128,4096]{1,0:T(8,128)(2,1)S(1)}, f32[64,64]{1,0:T(8,128)S(1)}) custom-call(f32[64,4096]{1,0:T(8,128)S(1)} %copy-done.2), custom_call_target="tpu_custom_call" | custom-call | tf_op jit(solution)/shard_map/modes/pallas_call | solution.py:443
  14.0 0.0 copy-start
  14.0 1.0 %copy-done = bf16[128,4096]{1,0:T(8,128)(2,1)} copy-done((bf16[128,4096]{1,0:T(8,128)(2,1)}, bf16[128,4096]{1,0:T(8,128)(2,1)S(1)}, u32[]{:S(2)}) %copy-start) | copy-done | bytes 1048600
  15.0 0.0 copy-done.4
  15.0 0.1 copy.8.ids_ref
  15.1 5.2 %all-to-all-done = bf16[8,8,4096]{2,0,1:T(8,128)(2,1)S(1)} async-done(((bf16[8,8,4096]{2,0,1:T(8,128)(2,1)}), bf16[8,8,4096]{2,0,1:T(8,128)(2,1)S(1)}, u32[]{:S(2)}, u32[]{:S(2)}) %all-to-all-start) | async-done | bytes 524320 | tf_op jit(solution)/shard_map/all_to_all | solution.py:531
  20.3 0.0 copy-start.1
  20.3 0.0 copy-start.3
  20.3 1.6 %columns.1 = (bf16[32,4096]{1,0:T(8,128)(2,1)S(1)}, f32[1,64,128]{2,1,0:T(8,128)S(1)}) custom-call(s32[32,1]{1,0:T(8,128)S(1)} %copy.8.ids_ref, bf16[64,4096]{1,0:T(8,128)(2,1)S(1)} %bitcast.8, bf16[256,4096]{1,0:T(8,128)(2,1)S(1)} %get-tuple-element.12.parts, f32[64,1]{1,0:T(8,128)S(1)} %get-tuple-element.13.scale_ref, f32[64,64]{1,0:T(8,128)S(1)} %get-tuple-element.14.gram_ref), custom_call_target="tpu_custom_call" | custom-call | tf_op jit(solution)/shard_map/columns/pallas_call | solution.py:461
  21.9 2.5 %all_gather.6.both_ref = f32[2,64,128]{2,1,0:T(8,128)S(1)} all-gather(f32[1,64,128]{2,1,0:T(8,128)S(1)} %get-tuple-element.15), channel_id=1, replica_groups=mesh['y'=8,'z'=8,'x'=4,'c'=2] {'c'}, dimensions={0}, use_global_device_ids=true | all-gather | bytes 98304 | tf_op jit(solution)/shard_map/all_gather | solution.py:535
  24.3 0.1 half.1
  24.4 10.7 %all_to_all.34.parts_ref = f32[8,32,128]{2,1,0:T(8,128)S(1)} all-to-all(f32[8,32,128]{2,1,0:T(8,128)S(1)} %half.1), channel_id=1, replica_groups=mesh['y'=8,'z'=8,'x'=4,'c'=2] {'y'}, dimensions={0} | all-to-all | bytes 262144 | tf_op jit(solution)/shard_map/all_to_all | solution.py:519
  35.2 0.1 add.3
  35.3 17.2 %all_to_all.35.parts_ref = f32[8,32,128]{2,1,0:T(8,128)S(1)} all-to-all(f32[8,32,128]{2,1,0:T(8,128)S(1)} %add.3), channel_id=1, replica_groups=mesh['y'=8,'z'=8,'x'=4,'c'=2] {'z'}, dimensions={0} | all-to-all | bytes 262144 | tf_op jit(solution)/shard_map/all_to_all | solution.py:519
  52.5 0.1 add.4
  52.6 6.8 %all_to_all.36.parts_ref = f32[4,32,128]{2,1,0:T(8,128)S(1)} all-to-all(f32[4,32,128]{2,1,0:T(8,128)S(1)} %add.4), channel_id=1, replica_groups=mesh['y'=8,'z'=8,'x'=4,'c'=2] {'x'}, dimensions={0} | all-to-all | bytes 131072 | tf_op jit(solution)/shard_map/all_to_all | solution.py:519
  59.4 0.1 add.5
  59.5 6.0 %all_gather.7.packed_ref = f32[1,64,128]{2,1,0:T(8,128)S(1)} all-gather(f32[1,32,128]{2,1,0:T(8,128)S(1)} %add.5), channel_id=1, replica_groups=mesh['y'=8,'z'=8,'x'=4,'c'=2] {'c'}, dimensions={1}, use_global_device_ids=true | all-gather | bytes 49152 | tf_op jit(solution)/shard_map/all_gather | solution.py:540
  65.5 0.0 copy-done.1
  65.5 0.0 copy-done.3
  65.5 6.8 %finish.1 = (f32[96,4096]{1,0:T(8,128)}, f32[96,96]{1,0:T(8,128)}, f32[1,32]{1,0:T(1,128)}) custom-call(f32[1,64,128]{2,1,0:T(8,128)S(1)} %all_gather.7.packed_ref, f32[1,64]{1,0:T(1,128)S(1)} %bitcast.9, bf16[128,4096]{1,0:T(8,128)(2,1)S(1)} %copy-done.1, bf16[32,4096]{1,0:T(8,128)(2,1)S(1)} %get-tuple-element.17.columns), custom_call_target="tpu_custom_call" | custom-call | tf_op jit(solution)/shard_map/finish/pallas_call | solution.py:503
Async XLA Ops:
  0.6 14.4 %copy-start.4 = (s32[32]{0:T(128)S(1)}, s32[32]{0:T(128)}, u32[]{:S(2)}) copy-start(s32[32]{0:T(128)} %param.7) | copy-start | bytes 388
  0.6 19.6 %all-to-all-start = ((bf16[8,8,4096]{2,0,1:T(8,128)(2,1)}), bf16[8,8,4096]{2,0,1:T(8,128)(2,1)S(1)}, u32[]{:S(2)}, u32[]{:S(2)}) async-start(bf16[8,8,4096]{2,0,1:T(8,128)(2,1)} %bitcast.10), calls=%async_computation | async-start | bytes 1048576 | tf_op jit(solution)/shard_map/all_to_all | solution.py:531
  10.9 1.2 %copy-start.2 = (f32[64,4096]{1,0:T(8,128)S(1)}, f32[64,4096]{1,0:T(8,128)}, u32[]{:S(2)}) copy-start(f32[64,4096]{1,0:T(8,128)} %basis_ref.1) | copy-start | bytes 3145732
  14.0 1.0 %copy-start = (bf16[128,4096]{1,0:T(8,128)(2,1)}, bf16[128,4096]{1,0:T(8,128)(2,1)S(1)}, u32[]{:S(2)}) copy-start(bf16[128,4096]{1,0:T(8,128)(2,1)S(1)} %get-tuple-element.16.pair) | copy-start | bytes 3145732
  20.3 45.3 %copy-start.1 = (bf16[128,4096]{1,0:T(8,128)(2,1)S(1)}, bf16[128,4096]{1,0:T(8,128)(2,1)}, u32[]{:S(2)}) copy-start(bf16[128,4096]{1,0:T(8,128)(2,1)} %copy-done) | copy-start | bytes 3145732
  20.3 45.3 %copy-start.3 = (f32[64]{0:T(128)S(1)}, f32[64]{0:T(128)}, u32[]{:S(2)}) copy-start(f32[64]{0:T(128)} %param.5) | copy-start | bytes 772

commit v6 on v5

--- a/solution.py
+++ b/solution.py
@@ -399,7 +399,10 @@
 ):
     modes = values_ref.shape[1]
     lanes = pair.shape[1]
-    weights, projector, novelty = dense(packed_ref[0], values_ref[...], total_rows)
+    senders, rows = packed_ref.shape[0] // 2, packed_ref.shape[1]
+    top = sum_pairs(lambda index: packed_ref[2 * index], senders, 0, rows)
+    low = sum_pairs(lambda index: packed_ref[2 * index + 1], senders, 1, rows)
+    weights, projector, novelty = dense(jnp.concatenate([top, low], axis=0), values_ref[...], total_rows)
     rounded = weights.astype(BF16)
     rest = (weights - rounded.astype(F32)).astype(BF16)
     left = jnp.concatenate(
@@ -535,9 +538,8 @@
     both = near(lax.all_gather(packed, "c", axis=0, tiled=True))
     packed = take_half(place, both, lax.axis_size("y"))
     packed = add_up(place, exchange(packed, ("y",)), lax.axis_size("z"))
-    packed = add_up(place, exchange(packed, ("z",)), lax.axis_size("x"))
-    packed = add_up(place, exchange(packed, ("x",)), 1)
-    packed = near(lax.all_gather(packed, "c", axis=1, tiled=True))
+    packed = add_up(place, exchange(packed, ("z",)), lax.axis_size("x") * lax.axis_size("c"))
+    packed = exchange(packed, ("x", "c"))
     filtered, projector, novelty = finish(total_rows, packed, near(values[None, :]), pair, columns)
     return (filtered, projector, novelty.reshape(-1))
 

time: 72.7 us -> 70.8 us (0.974)
  blocking collectives: 43.3 us -> 41.5 us
    all_gather x1 -> x0, blocking collectives: 6.03 us -> none  [per_device(): packed = near(lax.all_gather(packed, 'c', axis=1, tiled=True))]
    all_to_all x3, blocking collectives: 34.8 us -> 39 us  [exchange(): return near(lax.all_to_all(copies, axes, 0, 0, tiled=True))]
where the time goes in v6:
time: 70.8 us; the launch traced here: 70.5 us
  blocking collectives  41.5 us (59%)
  Pallas kernels  10.7 us (15%)
  starting transfers between devices  10.2 us (14%)
  waiting for transfers between devices  5.17 us (7%)
  local copies, waits for them, and re-layouts  2.29 us (3%)
    all_to_all x3, blocking collectives, exchange(): return near(lax.all_to_all(copies, axes, 0, 0, tiled=True))  39 us
    all_to_all x1, starting transfers between devices, per_device(): lax.all_to_all(archive, ('x', 'c'), split_axis=1, concat_axis=0, tiled=True)  10.2 us
    pallas_call x1, Pallas kernels, finish(): pl.pallas_call(functools.partial(finish_kernel, total_rows), out_shape=(s...  6.89 us
    all_to_all x1, waiting for transfers between devices, per_device(): lax.all_to_all(archive, ('x', 'c'), split_axis=1, concat_axis=0, tiled=True)  5.17 us
    all_gather x1, blocking collectives, per_device(): both = near(lax.all_gather(packed, 'c', axis=0, tiled=True))  2.47 us
    unnamed x10, local copies, waits for them, and re-layouts  2.2 us
    pallas_call x1, Pallas kernels, prepare(): pl.pallas_call(functools.partial(modes_kernel, share), out_shape=(kept((M...  1.91 us
    pallas_call x1, Pallas kernels, gather(): pl.pallas_call(columns_kernel, out_shape=(kept((count, lanes), BF16), kep...  1.58 us
  transfers between devices with their start and end apart: 1, of which 1 were waited for; matrix products, arithmetic and copies ran while one was open for 0% of the time, Pallas kernels for 3%

profile of v6, /device:TPU:1, one launch (start us, length us, event | category | flops | bytes accessed | tf_op | source)
XLA Modules:
  0.0 70.5 jit_solution(6212444277017911432)
XLA Ops:
  0.6 0.0 copy-start.4
  0.6 10.2 %all-to-all-start = ((bf16[8,8,4096]{2,0,1:T(8,128)(2,1)}), bf16[8,8,4096]{2,0,1:T(8,128)(2,1)S(1)}, u32[]{:S(2)}, u32[]{:S(2)}) async-start(bf16[8,8,4096]{2,0,1:T(8,128)(2,1)} %bitcast.10), calls=%async_computation | async-start | bytes 1048576 | tf_op jit(solution)/shard_map/all_to_all | solution.py:534
  10.9 0.0 copy-start
  10.9 1.2 %copy-done = f32[64,4096]{1,0:T(8,128)S(1)} copy-done((f32[64,4096]{1,0:T(8,128)S(1)}, f32[64,4096]{1,0:T(8,128)}, u32[]{:S(2)}) %copy-start) | copy-done | bytes 1048600
  12.1 1.9 %modes.1 = (bf16[256,4096]{1,0:T(8,128)(2,1)S(1)}, f32[64,1]{1,0:T(8,128)S(1)}, bf16[128,4096]{1,0:T(8,128)(2,1)S(1)}, f32[64,64]{1,0:T(8,128)S(1)}) custom-call(f32[64,4096]{1,0:T(8,128)S(1)} %copy-done), custom_call_target="tpu_custom_call" | custom-call | tf_op jit(solution)/shard_map/modes/pallas_call | solution.py:446
  14.0 0.0 copy-start.1
  14.0 1.0 %copy-done.1 = bf16[128,4096]{1,0:T(8,128)(2,1)} copy-done((bf16[128,4096]{1,0:T(8,128)(2,1)}, bf16[128,4096]{1,0:T(8,128)(2,1)S(1)}, u32[]{:S(2)}) %copy-start.1) | copy-done | bytes 1048600
  15.0 0.0 copy-done.4
  15.0 0.1 copy.8.ids_ref
  15.1 5.2 %all-to-all-done = bf16[8,8,4096]{2,0,1:T(8,128)(2,1)S(1)} async-done(((bf16[8,8,4096]{2,0,1:T(8,128)(2,1)}), bf16[8,8,4096]{2,0,1:T(8,128)(2,1)S(1)}, u32[]{:S(2)}, u32[]{:S(2)}) %all-to-all-start) | async-done | bytes 524320 | tf_op jit(solution)/shard_map/all_to_all | solution.py:534
  20.3 0.0 copy-start.2
  20.3 0.0 copy-start.3
  20.3 1.6 %columns.1 = (bf16[32,4096]{1,0:T(8,128)(2,1)S(1)}, f32[1,64,128]{2,1,0:T(8,128)S(1)}) custom-call(s32[32,1]{1,0:T(8,128)S(1)} %copy.8.ids_ref, bf16[64,4096]{1,0:T(8,128)(2,1)S(1)} %bitcast.8, bf16[256,4096]{1,0:T(8,128)(2,1)S(1)} %get-tuple-element.12.parts, f32[64,1]{1,0:T(8,128)S(1)} %get-tuple-element.13.scale_ref, f32[64,64]{1,0:T(8,128)S(1)} %get-tuple-element.14.gram_ref), custom_call_target="tpu_custom_call" | custom-call | tf_op jit(solution)/shard_map/columns/pallas_call | solution.py:464
  21.9 2.5 %all_gather.3.both_ref = f32[2,64,128]{2,1,0:T(8,128)S(1)} all-gather(f32[1,64,128]{2,1,0:T(8,128)S(1)} %get-tuple-element.15), channel_id=1, replica_groups=mesh['y'=8,'z'=8,'x'=4,'c'=2] {'c'}, dimensions={0}, use_global_device_ids=true | all-gather | bytes 98304 | tf_op jit(solution)/shard_map/all_gather | solution.py:538
  24.3 0.1 half.1
  24.4 10.7 %all_to_all.34.parts_ref = f32[8,32,128]{2,1,0:T(8,128)S(1)} all-to-all(f32[8,32,128]{2,1,0:T(8,128)S(1)} %half.1), channel_id=1, replica_groups=mesh['y'=8,'z'=8,'x'=4,'c'=2] {'y'}, dimensions={0} | all-to-all | bytes 262144 | tf_op jit(solution)/shard_map/all_to_all | solution.py:522
  35.1 0.1 add.2
  35.2 17.2 %all_to_all.35.parts_ref = f32[8,32,128]{2,1,0:T(8,128)S(1)} all-to-all(f32[8,32,128]{2,1,0:T(8,128)S(1)} %add.2), channel_id=1, replica_groups=mesh['y'=8,'z'=8,'x'=4,'c'=2] {'z'}, dimensions={0} | all-to-all | bytes 262144 | tf_op jit(solution)/shard_map/all_to_all | solution.py:522
  52.5 0.1 add.3
  52.6 11.0 %all_to_all.36.packed_ref = f32[8,32,128]{2,1,0:T(8,128)S(1)} all-to-all(f32[8,32,128]{2,1,0:T(8,128)S(1)} %add.3), channel_id=1, replica_groups=mesh['y'=8,'z'=8,'x'=4,'c'=2] {'x','c'}, dimensions={0} | all-to-all | bytes 262144 | tf_op jit(solution)/shard_map/all_to_all | solution.py:522
  63.6 0.0 copy-done.2
  63.6 0.0 copy-done.3
  63.6 6.9 %finish.1 = (f32[96,4096]{1,0:T(8,128)}, f32[96,96]{1,0:T(8,128)}, f32[1,32]{1,0:T(1,128)}) custom-call(f32[8,32,128]{2,1,0:T(8,128)S(1)} %all_to_all.36.packed_ref, f32[1,64]{1,0:T(1,128)S(1)} %bitcast.9, bf16[128,4096]{1,0:T(8,128)(2,1)S(1)} %copy-done.2, bf16[32,4096]{1,0:T(8,128)(2,1)S(1)} %get-tuple-element.17.columns), custom_call_target="tpu_custom_call" | custom-call | tf_op jit(solution)/shard_map/finish/pallas_call | solution.py:506
Async XLA Ops:
  0.6 14.4 %copy-start.4 = (s32[32]{0:T(128)S(1)}, s32[32]{0:T(128)}, u32[]{:S(2)}) copy-start(s32[32]{0:T(128)} %param.7) | copy-start | bytes 388
  0.6 19.6 %all-to-all-start = ((bf16[8,8,4096]{2,0,1:T(8,128)(2,1)}), bf16[8,8,4096]{2,0,1:T(8,128)(2,1)S(1)}, u32[]{:S(2)}, u32[]{:S(2)}) async-start(bf16[8,8,4096]{2,0,1:T(8,128)(2,1)} %bitcast.10), calls=%async_computation | async-start | bytes 1048576 | tf_op jit(solution)/shard_map/all_to_all | solution.py:534
  10.9 1.2 %copy-start = (f32[64,4096]{1,0:T(8,128)S(1)}, f32[64,4096]{1,0:T(8,128)}, u32[]{:S(2)}) copy-start(f32[64,4096]{1,0:T(8,128)} %basis_ref.1) | copy-start | bytes 3145732
  14.0 1.0 %copy-start.1 = (bf16[128,4096]{1,0:T(8,128)(2,1)}, bf16[128,4096]{1,0:T(8,128)(2,1)S(1)}, u32[]{:S(2)}) copy-start(bf16[128,4096]{1,0:T(8,128)(2,1)S(1)} %get-tuple-element.16.pair) | copy-start | bytes 3145732
  20.3 43.4 %copy-start.2 = (bf16[128,4096]{1,0:T(8,128)(2,1)S(1)}, bf16[128,4096]{1,0:T(8,128)(2,1)}, u32[]{:S(2)}) copy-start(bf16[128,4096]{1,0:T(8,128)(2,1)} %copy-done.1) | copy-start | bytes 3145732
  20.3 43.4 %copy-start.3 = (f32[64]{0:T(128)S(1)}, f32[64]{0:T(128)}, u32[]{:S(2)}) copy-start(f32[64]{0:T(128)} %param.5) | copy-start | bytes 772
